TPU v7x, 128 devices: a whole 4x4x4 slice. The times are simulated.
128 devices in a mesh: seq: 32 (over y_lo, z, x), head: 4 (over y_hi, core).
Axes of the slice: x: 4, y: 4 (y_hi: 2, y_lo: 2; y = y_hi * 2 + y_lo), z: 4, core: 2. Of those that a mesh axis runs over, the one named last changes fastest.
Arguments:
- tokens: bfloat16 [4096, 7168], P('seq', 'head'), may hold values from -6 to 6
- latent_down: bfloat16 [7168, 576], P('head'), may hold values from -0.0625 to 0.0625
- latent_gain: float32 [512], replicated, may hold values from 0.5 to 1.5
- query_nope: bfloat16 [4096, 8192], P('seq', 'head'), may hold values from -200 to 200
- query_rope: bfloat16 [4096, 4096], P('seq', 'head'), may hold values from -6 to 6
- key_up: bfloat16 [64, 128, 512], P('head'), may hold values from -0.5 to 0.5
- value_up: bfloat16 [64, 512, 128], P('head'), may hold values from -0.25 to 0.25
- prefix_latent: bfloat16 [2048, 576], P('seq'), may hold values from -6 to 6
- prefix_length: int32 [1], replicated, may hold values from 1024 to 2048
- page_table: int32 [256], replicated, may hold values from 0 to 255, each once
Outputs:
- attended: bfloat16 [4096, 8192], P('seq', 'head')
- decode_pool: bfloat16 [256, 9216], P('seq')
Inputs may be any that keep to these rules, and one draw needn't show every extreme that they name: The prefix rows from prefix_length[0] on are not live. `page_table`: A permutation of the 256 decode slots.
All inputs are finite; a program needn't handle non-finite values.
Results may differ from a plain program's by a relative error of at most 0.015.
Values may be sent and summed in bfloat16 or wider, within the bound.
A program may use at most 128 MiB of HBM per device.

v0:
```python
import jax
import jax.numpy as jnp
from jax import lax
from jax.sharding import PartitionSpec as P

LATENT = 512
ROPE = 64
NOPE = 128
VHEAD = 128
PAGE = 16


def sent_to_all(value, axis):
    copies = jnp.broadcast_to(value, (lax.axis_size(axis), *value.shape))
    return lax.all_to_all(copies, axis, split_axis=0, concat_axis=0, tiled=True)


def of_everyone(value, axis):
    return sent_to_all(value, axis).astype(jnp.float32).sum(axis=0)


def in_order(parts, dim):
    lengths = list(parts.shape[1:])
    lengths[dim] *= parts.shape[0]
    return jnp.moveaxis(parts, 0, dim).reshape(lengths)


def gather_directly(value, axis, dim):
    parts = sent_to_all(value, axis)
    return in_order(parts, dim)


def angles(positions):
    half_width = ROPE // 2
    frequency = 10000.0 ** (-jnp.arange(half_width, dtype=jnp.float32) / half_width)
    return positions.astype(jnp.float32)[:, None] * frequency[None, :]


def rotate(values, angle_table):
    half_width = values.shape[-1] // 2
    first = values[..., :half_width]
    second = values[..., half_width:]
    cosine = jnp.cos(angle_table)
    sinus = jnp.sin(angle_table)
    return jnp.concatenate(
        [first * cosine - second * sinus, first * sinus + second * cosine], axis=-1
    )


def finish(mixed, latent_gain, positions):
    latent = mixed[:, :LATENT]
    rope_part = mixed[:, LATENT:]
    normed = (
        latent * lax.rsqrt(jnp.mean(latent * latent, axis=1, keepdims=True) + 1e-06) * latent_gain
    )
    return jnp.concatenate(
        [normed.astype(jnp.bfloat16), rotate(rope_part, angles(positions)).astype(jnp.bfloat16)],
        axis=1,
    )


def per_device(
    tokens,
    latent_down,
    latent_gain,
    query_nope,
    query_rope,
    key_up,
    value_up,
    prefix_latent,
    prefix_length,
    page_table,
):
    row_count = tokens.shape[0]
    head_count = key_up.shape[0]
    row_width = LATENT + ROPE
    queries_dev = row_count * head_count
    seq_index = lax.axis_index("seq")
    offset = prefix_length[0]
    first_row = seq_index * row_count
    positions = offset + first_row + jnp.arange(row_count, dtype=jnp.int32)
    partial_terms = jnp.dot(tokens, latent_down, preferred_element_type=jnp.float32)
    mixed = of_everyone(partial_terms.astype(jnp.bfloat16), "head").astype(jnp.float32)
    new_keys = finish(mixed, latent_gain, positions)
    lifted = jnp.einsum(
        "thn,hnl->thl",
        query_nope.reshape(row_count, head_count, NOPE),
        key_up,
        preferred_element_type=jnp.float32,
    ).astype(jnp.bfloat16)
    turned = rotate(
        query_rope.reshape(row_count, head_count, ROPE).astype(jnp.float32),
        angles(positions)[:, None, :],
    ).astype(jnp.bfloat16)
    queries = jnp.concatenate([lifted, turned], axis=2).reshape(queries_dev, row_width)
    query_token = first_row + jnp.arange(queries_dev, dtype=jnp.int32) // head_count
    score_scale = (NOPE + ROPE) ** (-0.5)

    def attend(state, key_rows, live_mask):
        running_top, denominator, running = state
        scores = (
            lax.dot_general(
                key_rows, queries, (((1,), (1,)), ((), ())), preferred_element_type=jnp.float32
            )
            * score_scale
        )
        new_top = jnp.maximum(running_top, jnp.max(jnp.where(live_mask, scores, -1e30), axis=0))
        weights = jnp.where(live_mask, jnp.exp(scores - new_top[None, :]), 0.0)
        fading = jnp.exp(running_top - new_top)
        denominator = denominator * fading + jnp.sum(weights, axis=0)
        update = lax.dot_general(
            weights.astype(jnp.bfloat16),
            key_rows[:, :LATENT],
            (((0,), (0,)), ((), ())),
            preferred_element_type=jnp.float32,
        )
        return (new_top, denominator, running * fading[:, None] + update)

    def guarded(state, key_rows, live_mask):
        return attend(state, key_rows, live_mask)

    def sweep_keys(state, key_rows, live_rule):
        total_rows = key_rows.shape[0]
        blocks = key_rows.reshape(total_rows // 512, 512, row_width)
        starts = 512 * jnp.arange(total_rows // 512, dtype=jnp.int32)

        def advance(inner_state, block_pair):
            key_block, block_start = block_pair
            key_index = block_start + jnp.arange(512, dtype=jnp.int32)
            return (guarded(inner_state, key_block, live_rule(key_index)), None)

        state, unused = lax.scan(advance, state, (blocks, starts))
        return state

    def prefix_rule(key_index):
        return jnp.broadcast_to((key_index < offset)[:, None], (key_index.shape[0], queries_dev))

    def group_rule(key_index):
        return key_index[:, None] <= query_token[None, :]

    prefix_all = gather_directly(prefix_latent, "seq", 0)
    state = (
        jnp.full((queries_dev,), -1e30, jnp.float32),
        jnp.zeros((queries_dev,), jnp.float32),
        jnp.zeros((queries_dev, LATENT), jnp.float32),
    )
    state = sweep_keys(state, prefix_all, prefix_rule)
    pages_dev = row_count // PAGE
    page_width = PAGE * row_width
    all_keys = lax.all_gather(new_keys, "seq", axis=0, tiled=True)
    state = sweep_keys(state, all_keys, group_rule)
    axis_size = lax.axis_size("seq")
    targets = lax.dynamic_slice_in_dim(page_table, seq_index * pages_dev, pages_dev)
    slot_ids = jnp.arange(axis_size * pages_dev, dtype=jnp.int32)
    select = (slot_ids[:, None] == targets[None, :]).astype(jnp.bfloat16)
    outgoing = jnp.dot(
        select, new_keys.reshape(pages_dev, page_width), preferred_element_type=jnp.float32
    ).astype(jnp.bfloat16)
    incoming = lax.all_to_all(outgoing, "seq", split_axis=0, concat_axis=0, tiled=True)
    decode_pool = jnp.sum(
        incoming.reshape(axis_size, pages_dev, page_width), axis=0, dtype=jnp.float32
    )
    running_top, denominator, running = state
    attention = (
        (running / denominator[:, None]).astype(jnp.bfloat16).reshape(row_count, head_count, LATENT)
    )
    output = jnp.einsum("thl,hlv->thv", attention, value_up, preferred_element_type=jnp.float32)
    attended = output.astype(jnp.bfloat16).reshape(row_count, head_count * VHEAD)
    return (attended, decode_pool.astype(jnp.bfloat16))


def solution(mesh):
    placed = (
        P("seq", "head"),
        P("head", None),
        P(),
        P("seq", "head"),
        P("seq", "head"),
        P("head", None, None),
        P("head", None, None),
        P("seq", None),
        P(),
        P(),
    )
    return jax.shard_map(
        per_device,
        mesh=mesh,
        in_specs=placed,
        out_specs=(P("seq", "head"), P("seq", None)),
        check_vma=False,
    )
```

profile of v0, /device:TPU:104, one launch (start us, length us, event | category | flops | bytes accessed | tf_op | source)
XLA Modules:
  0.0 339.1 jit_solution(6677885738440692457)
XLA Ops:
  7.2 2.6 convolution_convert_fusion.1
  10.7 3.6 %all-to-all-start.1 = ((bf16[4,128,576]{1,2,0:T(8,128)(2,1)}), bf16[4,128,576]{1,2,0:T(8,128)(2,1)S(1)}, u32[]{:S(2)}, u32[]{:S(2)}) async-start(bf16[4,128,576]{1,2,0:T(8,128)(2,1)} %broadcast_in_dim.54), calls=%async_computation.1 | async-start | bytes 1179648 | tf_op jit(solution)/shard_map/all_to_all | solution.py:15
  15.1 10.1 %all-to-all-done.1 = bf16[4,128,576]{1,2,0:T(8,128)(2,1)S(1)} async-done(((bf16[4,128,576]{1,2,0:T(8,128)(2,1)}), bf16[4,128,576]{1,2,0:T(8,128)(2,1)S(1)}, u32[]{:S(2)}, u32[]{:S(2)}) %all-to-all-start.1) | async-done | bytes 589856 | tf_op jit(solution)/shard_map/all_to_all | solution.py:15
  25.3 2.7 broadcast_in_dim.53
  28.0 8.1 %all-to-all-start = ((bf16[32,64,576]{2,1,0:T(8,128)(2,1)}), bf16[32,64,576]{2,1,0:T(8,128)(2,1)}, u32[]{:S(2)}, u32[]{:S(2)}) async-start(bf16[32,64,576]{2,1,0:T(8,128)(2,1)} %broadcast_in_dim.53), calls=%async_computation | async-start | bytes 5242880 | tf_op jit(solution)/shard_map/all_to_all | solution.py:15
  36.2 3.2 convert_bitcast_fusion
  40.7 1.1 copy.46
  41.7 3.2 pad_maximum_fusion
  44.9 4.9 %copy.42 = bf16[128,16,576]{2,1,0:T(8,128)(2,1)} copy(bf16[128,16,576]{0,2,1:T(8,128)(2,1)} %pad_maximum_fusion) | data formatting | bytes 4718592 | tf_op jit(solution)/shard_map/concatenate | solution.py:95
  50.0 3.5 %fusion.30 = bf16[32,8,9216]{2,1,0:T(8,128)(2,1)} fusion(bf16[8,9216]{1,0:T(8,128)(2,1)S(1)} %reshape.119, s32[8]{0:T(128)S(1)} %dynamic_slice.19), kind=kOutput, calls=%fused_computation.47 | convolution fusion | flops 40110080 | bytes 4866080 | tf_op jit(solution)/shard_map/dot_general | solution.py:156
  53.5 19.3 %all-to-all-done = bf16[32,64,576]{2,1,0:T(8,128)(2,1)} async-done(((bf16[32,64,576]{2,1,0:T(8,128)(2,1)}), bf16[32,64,576]{2,1,0:T(8,128)(2,1)}, u32[]{:S(2)}, u32[]{:S(2)}) %all-to-all-start) | async-done | bytes 2359328 | tf_op jit(solution)/shard_map/all_to_all | solution.py:15
  72.8 8.4 %all-to-all-start.2 = ((bf16[32,8,9216]{2,1,0:T(8,128)(2,1)}), bf16[32,8,9216]{2,1,0:T(8,128)(2,1)}, u32[]{:S(2)}, u32[]{:S(2)}) async-start(bf16[32,8,9216]{2,1,0:T(8,128)(2,1)} %fusion.30), calls=%async_computation.2 | async-start | bytes 9437184 | tf_op jit(solution)/shard_map/all_to_all | solution.py:159
  81.2 65.6 %while.31 = (s32[]{:T(128)}, f32[2048]{0:T(1024)S(1)}, f32[2048]{0:T(1024)S(1)}, f32[2048,512]{1,0:T(8,128)}, s32[4]{0:T(128)S(1)}, /*index=5*/s32[]{:T(128)}, b...) while((s32[]{:T(128)}, f32[2048]{0:T(1024)S(1)}, ...), condition=%wide.region_3.4_spmd.clone, body=%wide.region_0.3_spmd.clone.sunk | while | flops 2296392704 | bytes 42535076 | solution.py:132
  81.8 1.2 add_compare_fusion.2
  83.0 1.2 dynamic-slice_bitcast_fusion.5
  84.1 5.7 %select_reduce_fusion.2 = (f32[2048]{0:T(1024)S(1)}, f32[512,2048]{1,0:T(8,128)}) fusion(pred[512]{0:T(512)(128)(4,1)S(1)} %add_compare_fusion.2, bf16[512,576]{1,0:T(8,128)(2,1)S(1)} %dynamic-slice_bitcast_fusion.5, bf16[2048,576]{1,0:T(8,128)(2,1)} %get-tuple-element.343), kind=kOutput, calls=%fused_computation.30.clone.1 | convolution fusion | flops 1211103232 | bytes 7152128 | tf_op jit(solution)/shard_map/while/body/eval_jaxpr/dot_general | solution.py:102
  89.9 3.2 fusion.74
  93.3 3.1 fusion.76
  96.9 1.2 add_compare_fusion.2
  98.2 1.2 dynamic-slice_bitcast_fusion.5
  99.3 5.7 %select_reduce_fusion.2 = (f32[2048]{0:T(1024)S(1)}, f32[512,2048]{1,0:T(8,128)}) fusion(pred[512]{0:T(512)(128)(4,1)S(1)} %add_compare_fusion.2, bf16[512,576]{1,0:T(8,128)(2,1)S(1)} %dynamic-slice_bitcast_fusion.5, bf16[2048,576]{1,0:T(8,128)(2,1)} %get-tuple-element.343), kind=kOutput, calls=%fused_computation.30.clone.1 | convolution fusion | flops 1211103232 | bytes 7152128 | tf_op jit(solution)/shard_map/while/body/eval_jaxpr/dot_general | solution.py:102
  105.0 3.2 fusion.74
  108.5 4.7 %fusion.76 = f32[2048,512]{1,0:T(8,128)} fusion(f32[2048,512]{1,0:T(8,128)} %get-tuple-element.329, f32[512,2048]{1,0:T(8,128)S(1)} %copy-done.1, f32[2048]{0:T(1024)S(1)} %get-tuple-element.315, f32[2048]{0:T(1024)S(1)} %select_maximum_fusion.2, pred[512]{0:T(512)(128)(4,1)S(1)} %add_compare_fusion.2, pred[]{:T(512)S(6)} %compare.5, ...), kind=kOutput, calls=%fused_computation.28.clone.1 | convolution fusion | flops 1081081856 | bytes 13124097 | tf_op jit(solution)/shard_map/while/body/eval_jaxpr/dot_general | solution.py:111
  113.7 1.2 add_compare_fusion.2
  114.9 1.2 dynamic-slice_bitcast_fusion.5
  116.1 5.7 %select_reduce_fusion.2 = (f32[2048]{0:T(1024)S(1)}, f32[512,2048]{1,0:T(8,128)}) fusion(pred[512]{0:T(512)(128)(4,1)S(1)} %add_compare_fusion.2, bf16[512,576]{1,0:T(8,128)(2,1)S(1)} %dynamic-slice_bitcast_fusion.5, bf16[2048,576]{1,0:T(8,128)(2,1)} %get-tuple-element.343), kind=kOutput, calls=%fused_computation.30.clone.1 | convolution fusion | flops 1211103232 | bytes 7152128 | tf_op jit(solution)/shard_map/while/body/eval_jaxpr/dot_general | solution.py:102
  121.8 3.2 fusion.74
  125.3 4.7 %fusion.76 = f32[2048,512]{1,0:T(8,128)} fusion(f32[2048,512]{1,0:T(8,128)} %get-tuple-element.329, f32[512,2048]{1,0:T(8,128)S(1)} %copy-done.1, f32[2048]{0:T(1024)S(1)} %get-tuple-element.315, f32[2048]{0:T(1024)S(1)} %select_maximum_fusion.2, pred[512]{0:T(512)(128)(4,1)S(1)} %add_compare_fusion.2, pred[]{:T(512)S(6)} %compare.5, ...), kind=kOutput, calls=%fused_computation.28.clone.1 | convolution fusion | flops 1081081856 | bytes 13124097 | tf_op jit(solution)/shard_map/while/body/eval_jaxpr/dot_general | solution.py:111
  130.5 1.2 add_compare_fusion.2
  131.7 1.2 dynamic-slice_bitcast_fusion.5
  132.9 5.7 %select_reduce_fusion.2 = (f32[2048]{0:T(1024)S(1)}, f32[512,2048]{1,0:T(8,128)}) fusion(pred[512]{0:T(512)(128)(4,1)S(1)} %add_compare_fusion.2, bf16[512,576]{1,0:T(8,128)(2,1)S(1)} %dynamic-slice_bitcast_fusion.5, bf16[2048,576]{1,0:T(8,128)(2,1)} %get-tuple-element.343), kind=kOutput, calls=%fused_computation.30.clone.1 | convolution fusion | flops 1211103232 | bytes 7152128 | tf_op jit(solution)/shard_map/while/body/eval_jaxpr/dot_general | solution.py:102
  138.6 3.2 fusion.74
  142.1 4.7 %fusion.76 = f32[2048,512]{1,0:T(8,128)} fusion(f32[2048,512]{1,0:T(8,128)} %get-tuple-element.329, f32[512,2048]{1,0:T(8,128)S(1)} %copy-done.1, f32[2048]{0:T(1024)S(1)} %get-tuple-element.315, f32[2048]{0:T(1024)S(1)} %select_maximum_fusion.2, pred[512]{0:T(512)(128)(4,1)S(1)} %add_compare_fusion.2, pred[]{:T(512)S(6)} %compare.5, ...), kind=kOutput, calls=%fused_computation.28.clone.1 | convolution fusion | flops 1081081856 | bytes 13124097 | tf_op jit(solution)/shard_map/while/body/eval_jaxpr/dot_general | solution.py:111
  146.7 7.8 %all-to-all-done.2 = bf16[32,8,9216]{2,1,0:T(8,128)(2,1)} async-done(((bf16[32,8,9216]{2,1,0:T(8,128)(2,1)}), bf16[32,8,9216]{2,1,0:T(8,128)(2,1)}, u32[]{:S(2)}, u32[]{:S(2)}) %all-to-all-start.2) | async-done | bytes 4718624 | tf_op jit(solution)/shard_map/all_to_all | solution.py:159
  154.5 3.7 %reduce_sum.50 = bf16[8,9216]{1,0:T(8,128)(2,1)} reduce(bf16[32,8,9216]{2,1,0:T(8,128)(2,1)} %all-to-all-done.2, bf16[]{:T(256)} %constant.81.clone.1), dimensions={0}, to_apply=%region_10.11 | reduce | flops 2285568 | bytes 4866050 | tf_op jit(solution)/shard_map/reduce_sum | solution.py:160
  158.2 66.2 %all-gather.2.cloned.1.call-done = bf16[4096,576]{0,1:T(8,128)(2,1)} async-done(((bf16[128,576]{0,1:T(8,128)(2,1)}), bf16[4096,576]{0,1:T(8,128)(2,1)}) %all-gather.2.cloned.1.call-update) | async-done | bytes 4718608 | tf_op jit(solution)/shard_map/all_gather | solution.py:150
  224.5 7.6 %copy.50 = bf16[4096,576]{1,0:T(8,128)(2,1)} copy(bf16[4096,576]{0,1:T(8,128)(2,1)} %all-gather.2.cloned.1.call-done) | data formatting | bytes 9437184
  232.1 93.6 %while.30 = (s32[]{:T(128)}, f32[2048]{0:T(1024)S(1)}, f32[2048]{0:T(1024)S(1)}, f32[2048,512]{1,0:T(8,128)}, s32[8]{0:T(128)S(1)}, /*index=5*/bf16[8,512,576]{2...) while((s32[]{:T(128)}, f32[2048]{0:T(1024)S(1)}, f32[2048]{0:T(1024)S(1)}, ...), condition=%wide.region_9.10_spmd.clone, body=%wide.region_6.9_spmd.clone.sunk | while | flops 2298501632 | bytes 25796724 | solution.py:132
  233.3 1.2 dynamic-slice_bitcast_fusion.4
  234.5 3.7 %fusion.68 = (f32[2048]{0:T(1024)S(1)}, f32[512,2048]{1,0:T(8,128)S(1)}) fusion(s32[2048]{0:T(1024)S(1)} %fusion.67, s32[512]{0:T(512)S(1)} %iota_add_fusion.2, bf16[512,576]{1,0:T(8,128)(2,1)S(1)} %dynamic-slice_bitcast_fusion.4, bf16[2048,576]{1,0:T(8,128)(2,1)} %get-tuple-element.370), kind=kOutput, calls=%fused_computation.3.clone.1 | convolution fusion | flops 1212151808 | bytes 7161856 | tf_op jit(solution)/shard_map/while/body/eval_jaxpr/dot_general | solution.py:102
  239.2 4.6 %multiply_add_fusion.5 = f32[2048,512]{1,0:T(8,128)} fusion(f32[2048,512]{1,0:T(8,128)} %get-tuple-element.358, f32[512,2048]{1,0:T(8,128)S(1)} %get-tuple-element.301, f32[2048]{0:T(1024)S(1)} %get-tuple-element.303, f32[2048]{0:T(1024)S(1)} %max.11, s32[2048]{0:T(1024)S(1)} %fusion.67, s32[512]{0:T(512)S(1)} %iota_add_fusion.2, ...), kind=kOutput, calls=%fused_computation.4.clone.1 | convolution fusion | flops 1081081856 | bytes 13133824 | tf_op jit(solution)/shard_map/while/body/eval_jaxpr/dot_general | solution.py:111
  245.0 1.2 dynamic-slice_bitcast_fusion.4
  246.2 3.7 %fusion.68 = (f32[2048]{0:T(1024)S(1)}, f32[512,2048]{1,0:T(8,128)S(1)}) fusion(s32[2048]{0:T(1024)S(1)} %fusion.67, s32[512]{0:T(512)S(1)} %iota_add_fusion.2, bf16[512,576]{1,0:T(8,128)(2,1)S(1)} %dynamic-slice_bitcast_fusion.4, bf16[2048,576]{1,0:T(8,128)(2,1)} %get-tuple-element.370), kind=kOutput, calls=%fused_computation.3.clone.1 | convolution fusion | flops 1212151808 | bytes 7161856 | tf_op jit(solution)/shard_map/while/body/eval_jaxpr/dot_general | solution.py:102
  250.9 4.6 %multiply_add_fusion.5 = f32[2048,512]{1,0:T(8,128)} fusion(f32[2048,512]{1,0:T(8,128)} %get-tuple-element.358, f32[512,2048]{1,0:T(8,128)S(1)} %get-tuple-element.301, f32[2048]{0:T(1024)S(1)} %get-tuple-element.303, f32[2048]{0:T(1024)S(1)} %max.11, s32[2048]{0:T(1024)S(1)} %fusion.67, s32[512]{0:T(512)S(1)} %iota_add_fusion.2, ...), kind=kOutput, calls=%fused_computation.4.clone.1 | convolution fusion | flops 1081081856 | bytes 13133824 | tf_op jit(solution)/shard_map/while/body/eval_jaxpr/dot_general | solution.py:111
  256.7 1.2 dynamic-slice_bitcast_fusion.4
  257.9 3.6 %fusion.68 = (f32[2048]{0:T(1024)S(1)}, f32[512,2048]{1,0:T(8,128)S(1)}) fusion(s32[2048]{0:T(1024)S(1)} %fusion.67, s32[512]{0:T(512)S(1)} %iota_add_fusion.2, bf16[512,576]{1,0:T(8,128)(2,1)S(1)} %dynamic-slice_bitcast_fusion.4, bf16[2048,576]{1,0:T(8,128)(2,1)} %get-tuple-element.370), kind=kOutput, calls=%fused_computation.3.clone.1 | convolution fusion | flops 1212151808 | bytes 7161856 | tf_op jit(solution)/shard_map/while/body/eval_jaxpr/dot_general | solution.py:102
  262.6 4.6 %multiply_add_fusion.5 = f32[2048,512]{1,0:T(8,128)} fusion(f32[2048,512]{1,0:T(8,128)} %get-tuple-element.358, f32[512,2048]{1,0:T(8,128)S(1)} %get-tuple-element.301, f32[2048]{0:T(1024)S(1)} %get-tuple-element.303, f32[2048]{0:T(1024)S(1)} %max.11, s32[2048]{0:T(1024)S(1)} %fusion.67, s32[512]{0:T(512)S(1)} %iota_add_fusion.2, ...), kind=kOutput, calls=%fused_computation.4.clone.1 | convolution fusion | flops 1081081856 | bytes 13133824 | tf_op jit(solution)/shard_map/while/body/eval_jaxpr/dot_general | solution.py:111
  268.4 1.2 dynamic-slice_bitcast_fusion.4
  269.6 3.6 %fusion.68 = (f32[2048]{0:T(1024)S(1)}, f32[512,2048]{1,0:T(8,128)S(1)}) fusion(s32[2048]{0:T(1024)S(1)} %fusion.67, s32[512]{0:T(512)S(1)} %iota_add_fusion.2, bf16[512,576]{1,0:T(8,128)(2,1)S(1)} %dynamic-slice_bitcast_fusion.4, bf16[2048,576]{1,0:T(8,128)(2,1)} %get-tuple-element.370), kind=kOutput, calls=%fused_computation.3.clone.1 | convolution fusion | flops 1212151808 | bytes 7161856 | tf_op jit(solution)/shard_map/while/body/eval_jaxpr/dot_general | solution.py:102
  274.3 4.6 %multiply_add_fusion.5 = f32[2048,512]{1,0:T(8,128)} fusion(f32[2048,512]{1,0:T(8,128)} %get-tuple-element.358, f32[512,2048]{1,0:T(8,128)S(1)} %get-tuple-element.301, f32[2048]{0:T(1024)S(1)} %get-tuple-element.303, f32[2048]{0:T(1024)S(1)} %max.11, s32[2048]{0:T(1024)S(1)} %fusion.67, s32[512]{0:T(512)S(1)} %iota_add_fusion.2, ...), kind=kOutput, calls=%fused_computation.4.clone.1 | convolution fusion | flops 1081081856 | bytes 13133824 | tf_op jit(solution)/shard_map/while/body/eval_jaxpr/dot_general | solution.py:111
  280.1 1.2 dynamic-slice_bitcast_fusion.4
  281.3 3.7 %fusion.68 = (f32[2048]{0:T(1024)S(1)}, f32[512,2048]{1,0:T(8,128)S(1)}) fusion(s32[2048]{0:T(1024)S(1)} %fusion.67, s32[512]{0:T(512)S(1)} %iota_add_fusion.2, bf16[512,576]{1,0:T(8,128)(2,1)S(1)} %dynamic-slice_bitcast_fusion.4, bf16[2048,576]{1,0:T(8,128)(2,1)} %get-tuple-element.370), kind=kOutput, calls=%fused_computation.3.clone.1 | convolution fusion | flops 1212151808 | bytes 7161856 | tf_op jit(solution)/shard_map/while/body/eval_jaxpr/dot_general | solution.py:102
  286.0 4.6 %multiply_add_fusion.5 = f32[2048,512]{1,0:T(8,128)} fusion(f32[2048,512]{1,0:T(8,128)} %get-tuple-element.358, f32[512,2048]{1,0:T(8,128)S(1)} %get-tuple-element.301, f32[2048]{0:T(1024)S(1)} %get-tuple-element.303, f32[2048]{0:T(1024)S(1)} %max.11, s32[2048]{0:T(1024)S(1)} %fusion.67, s32[512]{0:T(512)S(1)} %iota_add_fusion.2, ...), kind=kOutput, calls=%fused_computation.4.clone.1 | convolution fusion | flops 1081081856 | bytes 13133824 | tf_op jit(solution)/shard_map/while/body/eval_jaxpr/dot_general | solution.py:111
  291.8 1.2 dynamic-slice_bitcast_fusion.4
  293.0 3.6 %fusion.68 = (f32[2048]{0:T(1024)S(1)}, f32[512,2048]{1,0:T(8,128)S(1)}) fusion(s32[2048]{0:T(1024)S(1)} %fusion.67, s32[512]{0:T(512)S(1)} %iota_add_fusion.2, bf16[512,576]{1,0:T(8,128)(2,1)S(1)} %dynamic-slice_bitcast_fusion.4, bf16[2048,576]{1,0:T(8,128)(2,1)} %get-tuple-element.370), kind=kOutput, calls=%fused_computation.3.clone.1 | convolution fusion | flops 1212151808 | bytes 7161856 | tf_op jit(solution)/shard_map/while/body/eval_jaxpr/dot_general | solution.py:102
  297.7 4.6 %multiply_add_fusion.5 = f32[2048,512]{1,0:T(8,128)} fusion(f32[2048,512]{1,0:T(8,128)} %get-tuple-element.358, f32[512,2048]{1,0:T(8,128)S(1)} %get-tuple-element.301, f32[2048]{0:T(1024)S(1)} %get-tuple-element.303, f32[2048]{0:T(1024)S(1)} %max.11, s32[2048]{0:T(1024)S(1)} %fusion.67, s32[512]{0:T(512)S(1)} %iota_add_fusion.2, ...), kind=kOutput, calls=%fused_computation.4.clone.1 | convolution fusion | flops 1081081856 | bytes 13133824 | tf_op jit(solution)/shard_map/while/body/eval_jaxpr/dot_general | solution.py:111
  303.5 1.2 dynamic-slice_bitcast_fusion.4
  304.7 3.6 %fusion.68 = (f32[2048]{0:T(1024)S(1)}, f32[512,2048]{1,0:T(8,128)S(1)}) fusion(s32[2048]{0:T(1024)S(1)} %fusion.67, s32[512]{0:T(512)S(1)} %iota_add_fusion.2, bf16[512,576]{1,0:T(8,128)(2,1)S(1)} %dynamic-slice_bitcast_fusion.4, bf16[2048,576]{1,0:T(8,128)(2,1)} %get-tuple-element.370), kind=kOutput, calls=%fused_computation.3.clone.1 | convolution fusion | flops 1212151808 | bytes 7161856 | tf_op jit(solution)/shard_map/while/body/eval_jaxpr/dot_general | solution.py:102
  309.4 4.6 %multiply_add_fusion.5 = f32[2048,512]{1,0:T(8,128)} fusion(f32[2048,512]{1,0:T(8,128)} %get-tuple-element.358, f32[512,2048]{1,0:T(8,128)S(1)} %get-tuple-element.301, f32[2048]{0:T(1024)S(1)} %get-tuple-element.303, f32[2048]{0:T(1024)S(1)} %max.11, s32[2048]{0:T(1024)S(1)} %fusion.67, s32[512]{0:T(512)S(1)} %iota_add_fusion.2, ...), kind=kOutput, calls=%fused_computation.4.clone.1 | convolution fusion | flops 1081081856 | bytes 13133824 | tf_op jit(solution)/shard_map/while/body/eval_jaxpr/dot_general | solution.py:111
  315.2 1.2 dynamic-slice_bitcast_fusion.4
  316.4 3.7 %fusion.68 = (f32[2048]{0:T(1024)S(1)}, f32[512,2048]{1,0:T(8,128)S(1)}) fusion(s32[2048]{0:T(1024)S(1)} %fusion.67, s32[512]{0:T(512)S(1)} %iota_add_fusion.2, bf16[512,576]{1,0:T(8,128)(2,1)S(1)} %dynamic-slice_bitcast_fusion.4, bf16[2048,576]{1,0:T(8,128)(2,1)} %get-tuple-element.370), kind=kOutput, calls=%fused_computation.3.clone.1 | convolution fusion | flops 1212151808 | bytes 7161856 | tf_op jit(solution)/shard_map/while/body/eval_jaxpr/dot_general | solution.py:102
  321.1 4.6 %multiply_add_fusion.5 = f32[2048,512]{1,0:T(8,128)} fusion(f32[2048,512]{1,0:T(8,128)} %get-tuple-element.358, f32[512,2048]{1,0:T(8,128)S(1)} %get-tuple-element.301, f32[2048]{0:T(1024)S(1)} %get-tuple-element.303, f32[2048]{0:T(1024)S(1)} %max.11, s32[2048]{0:T(1024)S(1)} %fusion.67, s32[512]{0:T(512)S(1)} %iota_add_fusion.2, ...), kind=kOutput, calls=%fused_computation.4.clone.1 | convolution fusion | flops 1081081856 | bytes 13133824 | tf_op jit(solution)/shard_map/while/body/eval_jaxpr/dot_general | solution.py:111
  325.7 2.7 divide_convert_fusion
  328.5 2.7 fusion.33
  (111 shorter events, 25.0 us)
Async XLA Ops:
  7.2 29.1 %copy-start = (bf16[16,128,512]{2,1,0:T(8,128)(2,1)S(1)}, bf16[16,128,512]{2,1,0:T(8,128)(2,1)}, u32[]{:S(2)}) copy-start(bf16[16,128,512]{2,1,0:T(8,128)(2,1)} %param.19) | copy-start | bytes 6291460
  7.2 7.7 %copy-start.2 = (bf16[128,1024]{1,0:T(8,128)(2,1)S(1)}, bf16[128,1024]{1,0:T(8,128)(2,1)}, u32[]{:S(2)}) copy-start(bf16[128,1024]{1,0:T(8,128)(2,1)} %param.18) | copy-start | bytes 786436
  7.2 7.9 %copy-start.5 = (s32[256]{0:T(256)S(1)}, s32[256]{0:T(256)}, u32[]{:S(2)}) copy-start(s32[256]{0:T(256)} %param.23) | copy-start | bytes 3076
  10.7 14.6 %all-to-all-start.1 = ((bf16[4,128,576]{1,2,0:T(8,128)(2,1)}), bf16[4,128,576]{1,2,0:T(8,128)(2,1)S(1)}, u32[]{:S(2)}, u32[]{:S(2)}) async-start(bf16[4,128,576]{1,2,0:T(8,128)(2,1)} %broadcast_in_dim.54), calls=%async_computation.1 | async-start | bytes 1179648 | tf_op jit(solution)/shard_map/all_to_all | solution.py:15
  28.0 44.8 %all-to-all-start = ((bf16[32,64,576]{2,1,0:T(8,128)(2,1)}), bf16[32,64,576]{2,1,0:T(8,128)(2,1)}, u32[]{:S(2)}, u32[]{:S(2)}) async-start(bf16[32,64,576]{2,1,0:T(8,128)(2,1)} %broadcast_in_dim.53), calls=%async_computation | async-start | bytes 5242880 | tf_op jit(solution)/shard_map/all_to_all | solution.py:15
  36.1 3.6 %copy-start.3 = (f32[512]{0:T(512)S(1)}, f32[512]{0:T(512)}, u32[]{:S(2)}) copy-start(f32[512]{0:T(512)} %param.16) | copy-start | bytes 6148
  36.1 188.3 %all-gather.2.cloned.1.call-start = ((), (), s32[]{:S(2)}) async-start(), calls=%async_computation.3 | async-start | bytes 4866048 | tf_op jit(solution)/shard_map/all_gather | solution.py:150
  72.8 81.7 %all-to-all-start.2 = ((bf16[32,8,9216]{2,1,0:T(8,128)(2,1)}), bf16[32,8,9216]{2,1,0:T(8,128)(2,1)}, u32[]{:S(2)}, u32[]{:S(2)}) async-start(bf16[32,8,9216]{2,1,0:T(8,128)(2,1)} %fusion.30), calls=%async_computation.2 | async-start | bytes 9437184 | tf_op jit(solution)/shard_map/all_to_all | solution.py:159
  89.8 3.4 %copy-start.1 = (f32[512,2048]{1,0:T(8,128)S(1)}, f32[512,2048]{1,0:T(8,128)}, u32[]{:S(2)}) copy-start(f32[512,2048]{1,0:T(8,128)} %get-tuple-element.313) | copy-start | bytes 12582916 | tf_op jit(solution)/shard_map/while
  105.0 3.4 %copy-start.1 = (f32[512,2048]{1,0:T(8,128)S(1)}, f32[512,2048]{1,0:T(8,128)}, u32[]{:S(2)}) copy-start(f32[512,2048]{1,0:T(8,128)} %get-tuple-element.313) | copy-start | bytes 12582916 | tf_op jit(solution)/shard_map/while
  121.8 3.5 %copy-start.1 = (f32[512,2048]{1,0:T(8,128)S(1)}, f32[512,2048]{1,0:T(8,128)}, u32[]{:S(2)}) copy-start(f32[512,2048]{1,0:T(8,128)} %get-tuple-element.313) | copy-start | bytes 12582916 | tf_op jit(solution)/shard_map/while
  138.6 3.5 %copy-start.1 = (f32[512,2048]{1,0:T(8,128)S(1)}, f32[512,2048]{1,0:T(8,128)}, u32[]{:S(2)}) copy-start(f32[512,2048]{1,0:T(8,128)} %get-tuple-element.313) | copy-start | bytes 12582916 | tf_op jit(solution)/shard_map/while
  325.7 2.9 copy-start.4
Sparse Core Ops, SparseCore 0:
  40.7 183.7 all-gather.1
where the time goes:
time: 344 us; the launch traced here: 339 us
  matrix products  118 us (34%)
  waiting for transfers between devices  103 us (30%)
  other arithmetic  41.8 us (12%)
  local copies, waits for them, and re-layouts  40.6 us (12%)
  starting transfers between devices  20.2 us (6%)
  between operations  14.9 us (4%)
    all_gather x1, waiting for transfers between devices, per_device(): all_keys = lax.all_gather(new_keys, 'seq', axis=0, tiled=True)  66.2 us
    dot_general x12, matrix products, attend(): lax.dot_general(weights.astype(jnp.bfloat16), key_rows[:, :LATENT], (((0,...  53.9 us
    dot_general x12, matrix products, attend(): lax.dot_general(key_rows, queries, (((1,), (1,)), ((), ())), preferred_el...  52 us
    all_to_all x2, waiting for transfers between devices, sent_to_all(): return lax.all_to_all(copies, axis, split_axis=0, concat_axis=0, tiled=True)  29.4 us
    reduce_sum x12, other arithmetic, attend(): denominator = denominator * fading + jnp.sum(weights, axis=0)  20.7 us
    squeeze x12, local copies, waits for them, and re-layouts, sweep_keys(): state, unused = lax.scan(advance, state, (blocks, starts))  13.8 us
    all_to_all x2, starting transfers between devices, sent_to_all(): return lax.all_to_all(copies, axis, split_axis=0, concat_axis=0, tiled=True)  11.7 us
    unnamed x12, local copies, waits for them, and re-layouts  8.82 us
  transfers between devices with their start and end apart: 4, of which 4 were waited for; matrix products, arithmetic and copies ran while one was open for 25% of the time, Pallas kernels for 0%

commit v1 on v0

v1 whole, which is shorter than its diff:
```python
import functools
import jax
import jax.numpy as jnp
from jax import lax
from jax.experimental import pallas as pl
from jax.experimental.pallas import tpu as pltpu
from jax.sharding import PartitionSpec as P
LATENT, ROPE, NOPE, VHEAD, PAGE = 512, 64, 128, 128, 16
WIDTH = LATENT + ROPE
ORDERS = (("x", "y", "z"), ("y", "z", "x"), ("z", "x", "y"))
LANES = (pl.ds(0, 256), pl.ds(256, 256), pl.ds(512, 64))
ALL = slice(None)


def place(chip, core):
    y_hi, y_lo = chip["y"] // 2, chip["y"] % 2
    return {"seq": y_lo * 16 + chip["z"] * 4 + chip["x"], "head": y_hi * 2 + core}


def view(buf, chip, core, lanes):
    y = chip["y"]
    y_lo, y_hi = (ALL, ALL) if isinstance(y, slice) else (y % 2, y // 2)
    return buf.at[y_lo, chip["z"], chip["x"], y_hi, core, :, lanes]


class Spread:
    def __init__(self, buf, lanes, order, here, core, send, recv):
        self.buf, self.lanes, self.order = buf, lanes, order
        self.here, self.core, self.send, self.recv = here, core, send, recv

    def copy(self, chip, slot, to, core):
        ref = view(self.buf, chip, self.core, self.lanes)
        return pltpu.make_async_remote_copy(
            src_ref=ref, dst_ref=ref, send_sem=self.send.at[slot], recv_sem=self.recv.at[slot],
            device_id=place(to, core), device_id_type=pl.DeviceIdType.MESH)

    def landed(self, chip, slot):
        ref = view(self.buf, chip, self.core, self.lanes)
        pltpu.make_async_remote_copy(
            src_ref=ref, dst_ref=ref, send_sem=self.send.at[slot], recv_sem=self.recv.at[slot],
            device_id=place(self.here, 1 - self.core), device_id_type=pl.DeviceIdType.MESH).wait_recv()

    def shifted(self, dim, j):
        return {**self.here, dim: (self.here[dim] + j + 4) % 4}

    def group(self, depth, chip):
        return {**chip, **{d: ALL for d in self.order[:depth]}}

    def half(self, chip, k):
        dim = [d for d in self.order[:2] if d != "y"][0]
        return {**self.group(2, chip), dim: pl.ds(2 * k, 2)}

    def ring(self, depth):
        dim = self.order[depth]
        for j in (1, 3, 2):
            self.copy(self.group(depth, self.here), 3 * depth + j - 1, self.shifted(dim, j), self.core).start()

    def ring_landed(self, depth):
        dim = self.order[depth]
        for j in (1, 3, 2):
            self.landed(self.group(depth, self.shifted(dim, -j)), 3 * depth + j - 1)

    def last(self):
        dim = self.order[2]
        right, left = self.shifted(dim, 1), self.shifted(dim, -1)
        self.copy(self.half(self.here, 0), 6, right, self.core).start()
        self.copy(self.half(self.here, 1), 7, left, self.core).start()
        self.copy(self.half(self.here, 1), 8, right, self.core).start()
        self.copy(self.half(self.here, 0), 9, left, self.core).start()
        self.other(self.here, 12)

    def other(self, chip, slot):
        self.copy(self.group(2, chip), slot, self.here, 1 - self.core).start()

    def forward(self):
        dim = self.order[2]
        right, left = self.shifted(dim, 1), self.shifted(dim, -1)
        self.landed(self.half(left, 0), 6)
        self.copy(self.half(left, 0), 10, right, self.core).start()
        self.landed(self.half(right, 1), 7)
        self.copy(self.half(right, 1), 11, left, self.core).start()

    def sides(self):
        dim = self.order[2]
        right, left = self.shifted(dim, 1), self.shifted(dim, -1)
        self.landed(self.half(left, 1), 8)
        self.other(left, 13)
        self.landed(self.half(right, 0), 9)
        self.other(right, 14)

    def far(self):
        far = self.shifted(self.order[2], 2)
        self.landed(self.half(far, 0), 10)
        self.landed(self.half(far, 1), 11)
        self.other(far, 15)

    def others_landed(self):
        dim = self.order[2]
        for j, slot in ((0, 12), (-1, 13), (1, 14), (2, 15)):
            chip = self.group(2, self.shifted(dim, j))
            ref = view(self.buf, chip, 1 - self.core, self.lanes)
            pltpu.make_async_remote_copy(
                src_ref=ref, dst_ref=ref, send_sem=self.send.at[slot], recv_sem=self.recv.at[slot],
                device_id=place(self.here, 1 - self.core), device_id_type=pl.DeviceIdType.MESH).wait_recv()

    def sent(self):
        dim = self.order[2]
        right, left, far = self.shifted(dim, 1), self.shifted(dim, -1), self.shifted(dim, 2)
        for depth in (0, 1):
            for j in (1, 2, 3):
                self.copy(self.group(depth, self.here), 3 * depth + j - 1, self.shifted(self.order[depth], j), self.core).wait_send()
        for slot, chip, k, to in ((6, self.here, 0, right), (7, self.here, 1, left), (8, self.here, 1, right), (9, self.here, 0, left), (10, left, 0, right), (11, right, 1, left)):
            self.copy(self.half(chip, k), slot, to, self.core).wait_send()
        for slot, chip in ((12, self.here), (13, left), (14, right), (15, far)):
            self.copy(self.group(2, chip), slot, self.here, 1 - self.core).wait_send()


def position():
    seq, head = lax.axis_index("seq"), lax.axis_index("head")
    here = {"x": seq % 4, "y": (head // 2) * 2 + seq // 16, "z": (seq // 4) % 4}
    return here, head % 2, head


def greet(here, core):
    barrier = pltpu.get_barrier_semaphore()
    peers = [({**here, d: (here[d] + j) % 4}, core) for d in "xyz" for j in (1, 2, 3)]
    peers += [(here, 1 - core), ({**here, "y": (here["y"] + 2) % 4}, 1 - core)]
    for chip, c in peers:
        pl.semaphore_signal(barrier, inc=1, device_id=place(chip, c), device_id_type=pl.DeviceIdType.MESH)
    pl.semaphore_wait(barrier, len(peers))


def finish(mixed, gain, cos, sin):
    latent, a, b = mixed[:, :LATENT], mixed[:, LATENT : LATENT + 32], mixed[:, LATENT + 32 :]
    normed = latent * lax.rsqrt(jnp.mean(latent * latent, axis=1, keepdims=True) + 1e-06) * gain
    return jnp.concatenate([normed, a * cos - b * sin, a * sin + b * cos], axis=1).astype(jnp.bfloat16)


def gather_kernel(tok_ref, down_ref, gain_ref, cos_ref, sin_ref, pre_ref, pre_out, new_out,
                  pbuf, nbuf, part, parts, own_sem, send, recv, rs_send, rs_recv, out_sem):
    here, core, head = position()
    rows = nbuf.shape[5]
    prow = pbuf.shape[5]
    mine = (here["y"] % 2, here["z"], here["x"], here["y"] // 2, core)
    own = pltpu.make_async_copy(pre_ref.at[pl.ds(head * prow, prow), :], pbuf.at[mine], own_sem)
    own.start()
    greet(here, core)
    own.wait()
    pre = [Spread(pbuf, LANES[i], ORDERS[i], here, core, send.at[i], recv.at[i]) for i in range(3)]
    new = [Spread(nbuf, LANES[i], ORDERS[(i + 1) % 3], here, core, send.at[3 + i], recv.at[3 + i]) for i in range(3)]
    def each(group, name, *args):
        for item in group:
            getattr(item, name)(*args)
    each(pre, "ring", 0)
    term = jnp.dot(tok_ref[...], down_ref[...], preferred_element_type=jnp.float32)
    part[...] = term.astype(jnp.bfloat16)
    def share(j):
        to = (head + j) % 4
        return pltpu.make_async_remote_copy(
            src_ref=part.at[pl.ds(to * rows, rows), :], dst_ref=parts.at[j - 1], send_sem=rs_send.at[j - 1], recv_sem=rs_recv.at[j - 1],
            device_id={"seq": lax.axis_index("seq"), "head": to}, device_id_type=pl.DeviceIdType.MESH)
    for j in (1, 2, 3):
        share(j).start()
    each(pre, "ring_landed", 0)
    each(pre, "ring", 1)
    for j in (1, 2, 3):
        share(j).wait_recv()
    mixed = part[pl.ds(pl.multiple_of(head * rows, rows), rows), :].astype(jnp.float32)
    for j in range(3):
        mixed += parts[j].astype(jnp.float32)
    nbuf[mine] = finish(mixed, gain_ref[...], cos_ref[...], sin_ref[...])
    each(new, "ring", 0)
    each(pre, "ring_landed", 1)
    each(pre, "last")
    each(new, "ring_landed", 0)
    each(new, "ring", 1)
    each(pre, "forward")
    each(new, "ring_landed", 1)
    each(new, "last")
    each(pre, "sides")
    each(pre, "far")
    each(new, "forward")
    each(new, "sides")
    each(pre, "others_landed")
    out_p = pltpu.make_async_copy(pbuf, pre_out, out_sem.at[0])
    out_p.start()
    each(new, "far")
    each(new, "others_landed")
    out_n = pltpu.make_async_copy(nbuf, new_out, out_sem.at[1])
    out_n.start()
    each(pre, "sent")
    each(new, "sent")
    for j in (1, 2, 3):
        share(j).wait_send()
    out_p.wait()
    out_n.wait()


def gather(tokens, down, gain, cos, sin, prefix):
    rows, prow = tokens.shape[0] // 4, prefix.shape[0] // 4
    vm, hbm = pl.BlockSpec(memory_space=pltpu.VMEM), pl.BlockSpec(memory_space=pl.ANY)
    grid = (2, 4, 4, 2, 2)
    return pl.pallas_call(gather_kernel,
        out_shape=[jax.ShapeDtypeStruct((*grid, prow, WIDTH), jnp.bfloat16), jax.ShapeDtypeStruct((*grid, rows, WIDTH), jnp.bfloat16)],
        in_specs=[vm] * 5 + [hbm], out_specs=[hbm, hbm],
        scratch_shapes=[pltpu.VMEM((*grid, prow, WIDTH), jnp.bfloat16), pltpu.VMEM((*grid, rows, WIDTH), jnp.bfloat16),
            pltpu.VMEM((4 * rows, WIDTH), jnp.bfloat16), pltpu.VMEM((3, rows, WIDTH), jnp.bfloat16), pltpu.SemaphoreType.DMA,
            pltpu.SemaphoreType.DMA((6, 16)), pltpu.SemaphoreType.DMA((6, 16)), pltpu.SemaphoreType.DMA((3,)), pltpu.SemaphoreType.DMA((3,)), pltpu.SemaphoreType.DMA((2,))],
        compiler_params=pltpu.CompilerParams(vmem_limit_bytes=60 << 20, collective_id=0, has_side_effects=True), name="gather")(tokens, down, gain, cos, sin, prefix)


KB = 512
SCALE = (NOPE + ROPE) ** -0.5 * 1.4426950408889634
NEG = -1e30

def attn_kernel(heads, toks, n_pre, sc_ref, qn_ref, qr_ref, cos_ref, sin_ref, ku_ref, vu_ref, k_ref, out_ref, qt, acc, m_s, l_s, sb, vt):
    nq = heads * toks
    plen = sc_ref[0]
    first_row = sc_ref[1]
    pre_blocks = (plen + KB - 1) // KB
    own_blocks = (first_row + toks + KB - 1) // KB
    total = pre_blocks + own_blocks
    cos, sin = cos_ref[...], sin_ref[...]
    for h in range(heads):
        cols = pl.ds(h * toks, toks)
        lifted = jnp.dot(qn_ref[:, pl.ds(h * NOPE, NOPE)], ku_ref[h], preferred_element_type=jnp.float32)
        qt[:LATENT, cols] = lifted.T.astype(jnp.bfloat16)
    for g in range(heads // 2):
        both = qr_ref[:, pl.ds(g * 128, 128)].astype(jnp.float32).T
        for e in range(2):
            h = 2 * g + e
            a, b = both[64 * e : 64 * e + 32], both[64 * e + 32 : 64 * e + 64]
            cols = pl.ds(h * toks, toks)
            qt[LATENT : LATENT + 32, cols] = (a * cos - b * sin).astype(jnp.bfloat16)
            qt[LATENT + 32 :, cols] = (a * sin + b * cos).astype(jnp.bfloat16)
    m_s[...] = jnp.full_like(m_s, NEG)
    l_s[...] = jnp.zeros_like(l_s)
    acc[...] = jnp.zeros_like(acc)

    def row_of(i):
        return pl.multiple_of(jnp.where(i < pre_blocks, i * KB, n_pre + (i - pre_blocks) * KB), KB)

    def score(i, slot):
        keys = k_ref[pl.ds(row_of(i), KB), :]
        sb[slot] = jnp.dot(keys, qt[...], preferred_element_type=jnp.float32)
        in_pre = i < pre_blocks
        partial = jnp.logical_or(i == total - 1, i == pre_blocks - 1)
        @pl.when(partial)
        def _():
            for h in range(heads):
                cols = pl.ds(h * toks, toks)
                key = lax.broadcasted_iota(jnp.int32, (KB, toks), 0)
                tok = lax.broadcasted_iota(jnp.int32, (KB, toks), 1)
                limit = jnp.where(in_pre, plen - i * KB - 1, first_row - (i - pre_blocks) * KB)
                step = jnp.where(in_pre, 0, 1)
                sb[slot, :, cols] = jnp.where(key <= tok * step + limit, sb[slot, :, cols], NEG)

    def soft(i, slot):
        vt[...] = k_ref[pl.ds(row_of(i), KB), pl.ds(0, LATENT)].T
        s = sb[slot]
        old = m_s[0:1]
        new = jnp.maximum(old, jnp.max(s, axis=0, keepdims=True))
        fade = jnp.exp2((old - new) * SCALE)
        m_s[0:1] = new
        w = jnp.exp2((s - new) * SCALE)
        l_s[0:1] = l_s[0:1] * fade + jnp.sum(w, axis=0, keepdims=True)
        acc[...] = acc[...] * fade + jnp.dot(vt[...], w.astype(jnp.bfloat16), preferred_element_type=jnp.float32)

    score(0, 0)
    def step(pair, carry):
        for u in range(2):
            i = pair * 2 + u
            @pl.when(i < total)
            def _():
                score(jnp.minimum(i + 1, total - 1), 1 - u)
                soft(i, u)
        return carry
    lax.fori_loop(0, (total + 1) // 2, step, 0)
    for h in range(heads):
        cols = pl.ds(h * toks, toks)
        att = (acc[:, cols] / l_s[0:1, cols]).astype(jnp.bfloat16)
        out_ref[:, pl.ds(h * VHEAD, VHEAD)] = lax.dot_general(att, vu_ref[h], (((0,), (0,)), ((), ())), preferred_element_type=jnp.float32).astype(jnp.bfloat16)

def attend(scalars, qn, qr, cos, sin, ku, vu, keys, n_pre):
    heads, toks = ku.shape[0], qn.shape[0]
    nq = heads * toks
    vm = pl.BlockSpec(memory_space=pltpu.VMEM)
    return pl.pallas_call(functools.partial(attn_kernel, heads, toks, n_pre),
        out_shape=jax.ShapeDtypeStruct((toks, heads * VHEAD), jnp.bfloat16),
        in_specs=[pl.BlockSpec(memory_space=pltpu.SMEM)] + [vm] * 7, out_specs=vm,
        scratch_shapes=[pltpu.VMEM((LATENT + ROPE, nq), jnp.bfloat16), pltpu.VMEM((LATENT, nq), jnp.float32), pltpu.VMEM((8, nq), jnp.float32), pltpu.VMEM((8, nq), jnp.float32),
            pltpu.VMEM((2, KB, nq), jnp.float32), pltpu.VMEM((LATENT, KB), jnp.bfloat16)],
        compiler_params=pltpu.CompilerParams(vmem_limit_bytes=60 << 20), name="attend")(scalars, qn, qr, cos, sin, ku, vu, keys)


def tables(positions):
    frequency = 10000.0 ** (-jnp.arange(ROPE // 2, dtype=jnp.float32) / (ROPE // 2))
    angle = positions.astype(jnp.float32)[:, None] * frequency[None, :]
    return jnp.cos(angle), jnp.sin(angle)


def per_device(tokens, latent_down, latent_gain, query_nope, query_rope, key_up, value_up, prefix_latent, prefix_length, page_table):
    toks = tokens.shape[0]
    seq, head = lax.axis_index("seq"), lax.axis_index("head")
    offset = prefix_length[0]
    first_row = seq * toks
    cos, sin = tables(offset + first_row + jnp.arange(toks, dtype=jnp.int32))
    rows = toks // 4
    own_cos = lax.dynamic_slice_in_dim(cos, head * rows, rows)
    own_sin = lax.dynamic_slice_in_dim(sin, head * rows, rows)
    pre, new = gather(tokens, latent_down, latent_gain.reshape(1, LATENT), own_cos, own_sin, prefix_latent)
    keys = jnp.concatenate([pre.reshape(-1, WIDTH), new.reshape(-1, WIDTH)], axis=0)
    scalars = jnp.stack([offset, first_row])
    attended = attend(scalars, query_nope, query_rope, cos.T, sin.T, key_up, value_up, keys, 32 * prefix_latent.shape[0])
    pages = toks // PAGE
    slots = seq * pages + jnp.arange(pages, dtype=jnp.int32)
    wanted = jnp.sum(jnp.where(page_table[None, :] == slots[:, None], jnp.arange(page_table.shape[0], dtype=jnp.int32)[None, :], 0), axis=1)
    pool = new.reshape(page_table.shape[0], PAGE, WIDTH)[wanted].reshape(pages, PAGE * WIDTH)
    return attended, pool


def solution(mesh):
    placed = (P("seq", "head"), P("head", None), P(), P("seq", "head"), P("seq", "head"), P("head", None, None), P("head", None, None), P("seq", None), P(), P())
    return jax.shard_map(per_device, mesh=mesh, in_specs=placed, out_specs=(P("seq", "head"), P("seq", None)), check_vma=False)
```

time: 344 us -> 108 us (0.31)
  matrix products: 118 us -> 0 us
  waiting for transfers between devices: 103 us -> 0 us
  Pallas kernels: 0 us -> 87.3 us
  other arithmetic: 41.8 us -> 8.79 us
  local copies, waits for them, and re-layouts: 40.6 us -> 8.69 us
  starting transfers between devices: 20.2 us -> 0 us
  between operations: 14.9 us -> 1.33 us
    dot_general x28 -> x0, matrix products: 118 us -> none  [the longest x12 53.9 us: attend(): lax.dot_general(weights.astype(jnp.bfloat16), key_rows[:, :LATENT], (((0,...]
    pallas_call x0 -> x2, Pallas kernels: none -> 87.3 us  [the longest x1 51.8 us: attend(): pl.pallas_call(functools.partial(attn_kernel, heads, toks, n_pre), out_sh...]
    all_gather x1 -> x0, waiting for transfers between devices: 66.2 us -> none  [per_device(): all_keys = lax.all_gather(new_keys, 'seq', axis=0, tiled=True)]
    all_to_all x3 -> x0, waiting for transfers between devices: 37.2 us -> none  [the longest x2 29.4 us: sent_to_all(): return lax.all_to_all(copies, axis, split_axis=0, concat_axis=0, tiled=True)]
    reduce_sum x15 -> x1, other arithmetic: 24.6 us -> 0.18 us  [per_device(): jnp.sum(jnp.where(page_table[None, :] == slots[:, None], jnp.arange(page_...]
    all_to_all x3 -> x0, starting transfers between devices: 20.1 us -> none  [the longest x2 11.7 us: sent_to_all(): return lax.all_to_all(copies, axis, split_axis=0, concat_axis=0, tiled=True)]
    squeeze x12 -> x0, local copies, waits for them, and re-layouts: 13.8 us -> none  [sweep_keys(): state, unused = lax.scan(advance, state, (blocks, starts))]
    dynamic_slice x13 -> x0, local copies, waits for them, and re-layouts: 7.05 us -> none  [the longest x12 6.97 us: sweep_keys(): state, unused = lax.scan(advance, state, (blocks, starts))]
  transfers between devices with their start and end apart: 4 -> 0, of which waited for: 4 -> 0; matrix products, arithmetic and copies ran while one was open for 25% -> 0% of each run, Pallas kernels for 0% -> 0%
where the time goes in v1:
time: 108 us; the launch traced here: 106 us
  Pallas kernels  87.3 us (81%)
  other arithmetic  8.79 us (8%)
  local copies, waits for them, and re-layouts  8.69 us (8%)
  between operations  1.33 us (1%)
    pallas_call x1, Pallas kernels, attend(): pl.pallas_call(functools.partial(attn_kernel, heads, toks, n_pre), out_sh...  51.8 us
    pallas_call x1, Pallas kernels, gather(): pl.pallas_call(gather_kernel, out_shape=[jax.ShapeDtypeStruct((*grid, pro...  35.5 us
    concatenate x1, other arithmetic, per_device(): jnp.concatenate([pre.reshape(-1, WIDTH), new.reshape(-1, WIDTH)], axis=0)  7.1 us
    unnamed x3, local copies, waits for them, and re-layouts  4.1 us
    gather x1, local copies, waits for them, and re-layouts, per_device(): new.reshape(page_table.shape[0], PAGE, WIDTH)[wanted]  3.07 us

profile of v1, /device:TPU:104, one launch (start us, length us, event | category | flops | bytes accessed | tf_op | source)
XLA Modules:
  0.0 106.1 jit_solution(6729103115837256878)
XLA Ops:
  1.3 0.1 broadcast_multiply_fusion
  1.4 0.7 dynamic-slice_sine_fusion
  2.1 4.1 %copy.13.down_ref = bf16[1792,576]{1,0:T(8,128)(2,1)} copy(bf16[1792,576]{0,1:T(8,128)(2,1)} %param.11) | data formatting | bytes 4128768 | tf_op args[1]
  6.2 35.5 %gather.7 = (bf16[2,4,4,2,2,16,576]{6,5,4,3,2,1,0:T(8,128)(2,1)}, bf16[2,4,4,2,2,32,576]{6,5,4,3,2,1,0:T(8,128)(2,1)}) custom-call(bf16[128,1792]{1,0:T(8,128)(2,1)} %tok_ref.1, bf16[1792,576]{1,0:T(8,128)(2,1)} %copy.13.down_ref, f32[1,512]{1,0:T(1,128)} %bitcast.14, f32[32,32]{1,0:T(8,128)} %get-tuple-element.7.cos_ref, ...), custom_call_target="tpu_custom_call" | custom-call | tf_op jit(solution)/shard_map/gather/pallas_call | solution.py:203
  41.7 7.1 %pad_maximum_fusion.k_ref = bf16[6144,576]{1,0:T(8,128)(2,1)} fusion(bf16[4096,576]{1,0:T(8,128)(2,1)} %bitcast.11, bf16[2048,576]{1,0:T(8,128)(2,1)} %bitcast.13), kind=kLoop, calls=%fused_computation.1 | loop fusion | flops 14155776 | bytes 14155776 | tf_op jit(solution)/shard_map/concatenate | solution.py:312
  48.8 0.7 multiply_sine_fusion
  49.5 0.6 pad_add_fusion.sc_ref
  50.2 0.0 copy-start
  50.2 51.8 %attend.1 = bf16[128,2048]{1,0:T(8,128)(2,1)} custom-call(s32[2]{0:T(128)} %pad_add_fusion.sc_ref, bf16[128,2048]{1,0:T(8,128)(2,1)} %qn_ref.1, bf16[128,1024]{1,0:T(8,128)(2,1)} %qr_ref.1, f32[32,128]{1,0:T(8,128)} %get-tuple-element.9.cos_ref, f32[32,128]{1,0:T(8,128)} %get-tuple-element.8.sin_ref, bf16[16,128,512]{2,1,0:T(8,128)(2,1)} %ku_ref.1, ...), custom_call_target="tpu_custom_call" | custom-call | tf_op jit(solution)/shard_map/attend/pallas_call | solution.py:288
  102.0 0.0 copy-done
  102.0 0.2 select_reduce_fusion
  102.2 3.1 %gather_fusion = bf16[8,16,576]{2,1,0:T(8,128)(2,1)S(1)} fusion(bf16[256,16,576]{2,1,0:T(8,128)(2,1)} %bitcast.12, s32[1024]{0:T(1024)S(1)} %pad_clamp_fusion), kind=kCustom, calls=%fused_computation | custom fusion | bytes 294944 | tf_op jit(solution)/shard_map/gather | solution.py:318
  105.2 0.8 reshape.52
  (5 shorter events, 0.0 us)
Async XLA Ops:
  50.2 51.8 %copy-start = (s32[256]{0:T(256)S(1)}, s32[256]{0:T(256)}, u32[]{:S(2)}) copy-start(s32[256]{0:T(256)} %param.19) | copy-start | bytes 3076

commit v2 on v1

v2 whole, which is shorter than its diff:
```python
import functools
import jax
import jax.numpy as jnp
from jax import lax
from jax.experimental import pallas as pl
from jax.experimental.pallas import tpu as pltpu
from jax.sharding import PartitionSpec as P
LATENT, ROPE, NOPE, VHEAD, PAGE = 512, 64, 128, 128, 16
WIDTH = LATENT + ROPE
HALF = ROPE // 2
KB = 512
SCALE = (NOPE + ROPE) ** -0.5 * 1.4426950408889634
NEG = -1e30
ORDERS = (("x", "y", "z"), ("y", "z", "x"), ("z", "x", "y"))
LANES = (pl.ds(0, 256), pl.ds(256, 256), pl.ds(512, 64))
ALL = slice(None)


def place(chip, core):
    y_hi, y_lo = chip["y"] // 2, chip["y"] % 2
    return {"seq": y_lo * 16 + chip["z"] * 4 + chip["x"], "head": y_hi * 2 + core}


def view(buf, chip, core, lanes):
    y = chip["y"]
    y_lo, y_hi = (ALL, ALL) if isinstance(y, slice) else (y % 2, y // 2)
    return buf.at[y_lo, chip["z"], chip["x"], y_hi, core, :, lanes]


class Spread:
    def __init__(self, buf, lanes, order, here, core, send, recv):
        self.buf, self.lanes, self.order = buf, lanes, order
        self.here, self.core, self.send, self.recv = here, core, send, recv

    def copy(self, chip, slot, to, core):
        ref = view(self.buf, chip, self.core, self.lanes)
        return pltpu.make_async_remote_copy(
            src_ref=ref, dst_ref=ref, send_sem=self.send.at[slot], recv_sem=self.recv.at[slot],
            device_id=place(to, core), device_id_type=pl.DeviceIdType.MESH)

    def landed(self, chip, slot):
        ref = view(self.buf, chip, self.core, self.lanes)
        pltpu.make_async_remote_copy(
            src_ref=ref, dst_ref=ref, send_sem=self.send.at[slot], recv_sem=self.recv.at[slot],
            device_id=place(self.here, 1 - self.core), device_id_type=pl.DeviceIdType.MESH).wait_recv()

    def shifted(self, dim, j):
        return {**self.here, dim: (self.here[dim] + j + 4) % 4}

    def group(self, depth, chip):
        return {**chip, **{d: ALL for d in self.order[:depth]}}

    def half(self, chip, k):
        dim = [d for d in self.order[:2] if d != "y"][0]
        return {**self.group(2, chip), dim: pl.ds(2 * k, 2)}

    def ring(self, depth):
        dim = self.order[depth]
        for j in (1, 3, 2):
            self.copy(self.group(depth, self.here), 3 * depth + j - 1, self.shifted(dim, j), self.core).start()

    def ring_landed(self, depth):
        dim = self.order[depth]
        for j in (1, 3, 2):
            self.landed(self.group(depth, self.shifted(dim, -j)), 3 * depth + j - 1)

    def last(self):
        dim = self.order[2]
        right, left = self.shifted(dim, 1), self.shifted(dim, -1)
        self.copy(self.half(self.here, 0), 6, right, self.core).start()
        self.copy(self.half(self.here, 1), 7, left, self.core).start()
        self.copy(self.half(self.here, 1), 8, right, self.core).start()
        self.copy(self.half(self.here, 0), 9, left, self.core).start()
        self.other(self.here, 12)

    def other(self, chip, slot):
        self.copy(self.group(2, chip), slot, self.here, 1 - self.core).start()

    def forward(self):
        dim = self.order[2]
        right, left = self.shifted(dim, 1), self.shifted(dim, -1)
        self.landed(self.half(left, 0), 6)
        self.copy(self.half(left, 0), 10, right, self.core).start()
        self.landed(self.half(right, 1), 7)
        self.copy(self.half(right, 1), 11, left, self.core).start()

    def sides(self):
        dim = self.order[2]
        right, left = self.shifted(dim, 1), self.shifted(dim, -1)
        self.landed(self.half(left, 1), 8)
        self.other(left, 13)
        self.landed(self.half(right, 0), 9)
        self.other(right, 14)

    def far(self):
        far = self.shifted(self.order[2], 2)
        self.landed(self.half(far, 0), 10)
        self.landed(self.half(far, 1), 11)
        self.other(far, 15)

    def others_landed(self):
        dim = self.order[2]
        for j, slot in ((0, 12), (-1, 13), (1, 14), (2, 15)):
            chip = self.group(2, self.shifted(dim, j))
            ref = view(self.buf, chip, 1 - self.core, self.lanes)
            pltpu.make_async_remote_copy(
                src_ref=ref, dst_ref=ref, send_sem=self.send.at[slot], recv_sem=self.recv.at[slot],
                device_id=place(self.here, 1 - self.core), device_id_type=pl.DeviceIdType.MESH).wait_recv()

    def sent(self):
        dim = self.order[2]
        right, left, far = self.shifted(dim, 1), self.shifted(dim, -1), self.shifted(dim, 2)
        for depth in (0, 1):
            for j in (1, 2, 3):
                self.copy(self.group(depth, self.here), 3 * depth + j - 1, self.shifted(self.order[depth], j), self.core).wait_send()
        for slot, chip, k, to in ((6, self.here, 0, right), (7, self.here, 1, left), (8, self.here, 1, right), (9, self.here, 0, left), (10, left, 0, right), (11, right, 1, left)):
            self.copy(self.half(chip, k), slot, to, self.core).wait_send()
        for slot, chip in ((12, self.here), (13, left), (14, right), (15, far)):
            self.copy(self.group(2, chip), slot, self.here, 1 - self.core).wait_send()


def position():
    seq, head = lax.axis_index("seq"), lax.axis_index("head")
    here = {"x": seq % 4, "y": (head // 2) * 2 + seq // 16, "z": (seq // 4) % 4}
    return here, head % 2, head


def greet(here, core):
    barrier = pltpu.get_barrier_semaphore()
    peers = [({**here, d: (here[d] + j) % 4}, core) for d in "xyz" for j in (1, 2, 3)]
    peers += [(here, 1 - core), ({**here, "y": (here["y"] + 2) % 4}, 1 - core)]
    for chip, c in peers:
        pl.semaphore_signal(barrier, inc=1, device_id=place(chip, c), device_id_type=pl.DeviceIdType.MESH)
    pl.semaphore_wait(barrier, len(peers))


def finish(mixed, gain, cos, sin):
    latent, a, b = mixed[:, :LATENT], mixed[:, LATENT : LATENT + HALF], mixed[:, LATENT + HALF :]
    normed = latent * lax.rsqrt(jnp.mean(latent * latent, axis=1, keepdims=True) + 1e-06) * gain
    return jnp.concatenate([normed, a * cos - b * sin, a * sin + b * cos], axis=1).astype(jnp.bfloat16)


def each(group, name, *args):
    for item in group:
        getattr(item, name)(*args)


def kernel(heads, toks, len_ref, tab_ref, gain_ref, tok_hbm, down_hbm, pre_hbm, qn_hbm, qr_hbm, ku_hbm, vu_hbm,
           out_ref, pool_ref, pbuf, nbuf, part, parts, tok_ref, down_ref, qn_ref, qr_ref, ku_ref, vu_ref,
           qt, acc, m_s, l_s, sb, vt, in_sem, send, recv, rs_send, rs_recv):
    here, core, head = position()
    seq = lax.axis_index("seq")
    rows, prow = nbuf.shape[5], pbuf.shape[5]
    mine = (here["y"] % 2, here["z"], here["x"], here["y"] // 2, core)
    loads = [pltpu.make_async_copy(src, dst, in_sem.at[i]) for i, (src, dst) in enumerate((
        (pre_hbm.at[pl.ds(head * prow, prow), :], pbuf.at[mine]), (tok_hbm, tok_ref), (down_hbm, down_ref),
        (qn_hbm, qn_ref), (ku_hbm, ku_ref), (qr_hbm, qr_ref), (vu_hbm, vu_ref)))]
    for load in loads:
        load.start()
    greet(here, core)
    loads[0].wait()
    pre = [Spread(pbuf, LANES[i], ORDERS[i], here, core, send.at[i], recv.at[i]) for i in range(3)]
    new = [Spread(nbuf, LANES[i], ORDERS[(i + 1) % 3], here, core, send.at[3 + i], recv.at[3 + i]) for i in range(3)]
    each(pre, "ring", 0)

    loads[1].wait()
    loads[2].wait()
    term = lax.dot_general(tok_ref[...], down_ref[...], (((1,), (1,)), ((), ())), preferred_element_type=jnp.float32)
    part[...] = term.astype(jnp.bfloat16)

    def share(j):
        to = (head + j) % 4
        return pltpu.make_async_remote_copy(
            src_ref=part.at[pl.ds(to * rows, rows), :], dst_ref=parts.at[j - 1], send_sem=rs_send.at[j - 1], recv_sem=rs_recv.at[j - 1],
            device_id={"seq": seq, "head": to}, device_id_type=pl.DeviceIdType.MESH)

    for j in (1, 2, 3):
        share(j).start()
    each(pre, "ring_landed", 0)
    each(pre, "ring", 1)
    turn = tab_ref[...].T
    for j in (1, 2, 3):
        share(j).wait_recv()
    own_rows = pl.ds(pl.multiple_of(head * rows, rows), rows)
    mixed = part[own_rows, :].astype(jnp.float32)
    for j in range(3):
        mixed += parts[j].astype(jnp.float32)
    nbuf[mine] = finish(mixed, gain_ref[...], tab_ref[own_rows, :HALF], tab_ref[own_rows, HALF : 2 * HALF])
    each(new, "ring", 0)

    def lift(h):
        cols = pl.ds(h * toks, toks)
        lifted = jnp.dot(qn_ref[:, pl.ds(h * NOPE, NOPE)], ku_ref[h], preferred_element_type=jnp.float32)
        qt[:LATENT, cols] = lifted.T.astype(jnp.bfloat16)

    def rotate(g):
        cos, sin = turn[:HALF], turn[HALF : 2 * HALF]
        both = qr_ref[:, pl.ds(g * 2 * ROPE, 2 * ROPE)].astype(jnp.float32).T
        for e in range(2):
            a, b = both[ROPE * e : ROPE * e + HALF], both[ROPE * e + HALF : ROPE * (e + 1)]
            cols = pl.ds((2 * g + e) * toks, toks)
            qt[LATENT : LATENT + HALF, cols] = (a * cos - b * sin).astype(jnp.bfloat16)
            qt[LATENT + HALF :, cols] = (a * sin + b * cos).astype(jnp.bfloat16)

    loads[3].wait()
    loads[4].wait()
    for h in range(heads // 2):
        lift(h)
    each(pre, "ring_landed", 1)
    each(pre, "last")
    each(new, "ring_landed", 0)
    each(new, "ring", 1)
    for h in range(heads // 2, heads):
        lift(h)
    loads[5].wait()
    each(pre, "forward")
    for g in range(heads // 2):
        rotate(g)
    m_s[...] = jnp.full_like(m_s, NEG)
    l_s[...] = jnp.zeros_like(l_s)
    acc[...] = jnp.zeros_like(acc)
    each(new, "ring_landed", 1)
    each(new, "last")
    each(pre, "sides")
    each(pre, "far")
    each(pre, "others_landed")

    first_row = seq * toks
    own_blocks = (first_row + toks + KB - 1) // KB
    pre_blocks = pbuf.size // (WIDTH * KB)

    def pre_keys(b):
        return pbuf[b // 2, pl.ds(2 * (b % 2), 2)].reshape(KB, WIDTH)

    def new_keys(b):
        return nbuf[b // 4, b % 4].reshape(KB, WIDTH)

    def score(keys, slot):
        sb[slot] = jnp.dot(keys, qt[...], preferred_element_type=jnp.float32)

    def hide(slot, limit, step):
        for h in range(heads):
            cols = pl.ds(h * toks, toks)
            key = lax.broadcasted_iota(jnp.int32, (KB, toks), 0)
            tok = lax.broadcasted_iota(jnp.int32, (KB, toks), 1)
            sb[slot, :, cols] = jnp.where(key <= tok * step + limit, sb[slot, :, cols], NEG)

    def score_new(b, slot):
        score(new_keys(b), slot)
        @pl.when(b == own_blocks - 1)
        def _():
            hide(slot, first_row - b * KB, 1)

    def score_pre(b, slot):
        score(pre_keys(b), slot)
        if b >= 2:
            hide(slot, len_ref[0] - b * KB - 1, 0)

    def soft(keys, slot):
        vt[...] = keys[:, :LATENT].T
        s = sb[slot]
        old = m_s[0:1]
        top = jnp.maximum(old, jnp.max(s, axis=0, keepdims=True))
        fade = jnp.exp2((old - top) * SCALE)
        m_s[0:1] = top
        w = jnp.exp2((s - top) * SCALE)
        l_s[0:1] = l_s[0:1] * fade + jnp.sum(w, axis=0, keepdims=True)
        acc[...] = acc[...] * fade + jnp.dot(vt[...], w.astype(jnp.bfloat16), preferred_element_type=jnp.float32)

    score_pre(0, 0)
    score_pre(1, 1)
    soft(pre_keys(0), 0)
    each(new, "forward")
    score_pre(2, 0)
    soft(pre_keys(1), 1)
    each(new, "sides")
    score_pre(3, 1)
    soft(pre_keys(2), 0)
    each(new, "far")
    each(new, "others_landed")
    score_new(0, 0)
    soft(pre_keys(3), 1)

    def step(pair, carry):
        for u in range(2):
            b = pair * 2 + u
            @pl.when(b < own_blocks)
            def _():
                score_new(jnp.minimum(b + 1, own_blocks - 1), 1 - u)
                soft(new_keys(b), u)
        return carry

    lax.fori_loop(0, (own_blocks + 1) // 2, step, 0)

    wanted = tab_ref[:, 2 * HALF : 2 * HALF + 1]
    picked = jnp.zeros((toks, WIDTH), jnp.float32)
    for b in range(nbuf.size // (WIDTH * KB)):
        row = lax.broadcasted_iota(jnp.int32, (toks, KB), 1).astype(jnp.float32) + float(b * KB)
        pick = jnp.where(row == wanted, 1.0, 0.0).astype(jnp.bfloat16)
        picked += jnp.dot(pick, new_keys(b), preferred_element_type=jnp.float32)
    pool_ref[...] = picked.astype(jnp.bfloat16)
    loads[6].wait()
    for h in range(heads):
        cols = pl.ds(h * toks, toks)
        att = (acc[:, cols] / l_s[0:1, cols]).astype(jnp.bfloat16)
        out_ref[:, pl.ds(h * VHEAD, VHEAD)] = lax.dot_general(att, vu_ref[h], (((0,), (0,)), ((), ())), preferred_element_type=jnp.float32).astype(jnp.bfloat16)
    each(pre, "sent")
    each(new, "sent")
    for j in (1, 2, 3):
        share(j).wait_send()


def per_device(tokens, latent_down, latent_gain, query_nope, query_rope, key_up, value_up, prefix_latent, prefix_length, page_table):
    toks, heads = tokens.shape[0], key_up.shape[0]
    seq = lax.axis_index("seq")
    positions = prefix_length[0] + seq * toks + jnp.arange(toks, dtype=jnp.int32)
    frequency = 10000.0 ** (-jnp.arange(HALF, dtype=jnp.float32) / HALF)
    angle = positions.astype(jnp.float32)[:, None] * frequency[None, :]
    pages = toks // PAGE
    slots = seq * pages + jnp.arange(toks, dtype=jnp.int32) // PAGE
    count = page_table.shape[0]
    page = jnp.sum(jnp.where(page_table[None, :] == slots[:, None], jnp.arange(count, dtype=jnp.int32)[None, :], 0), axis=1)
    row = (page * PAGE + jnp.arange(toks, dtype=jnp.int32) % PAGE).astype(jnp.float32)
    table = jnp.concatenate([jnp.cos(angle), jnp.sin(angle), jnp.broadcast_to(row[:, None], (toks, 2 * HALF))], axis=1)
    rows, prow = toks // 4, prefix_latent.shape[0] // 4
    grid = (2, 4, 4, 2, 2)
    queries = heads * toks
    vm, sm, hbm = (pl.BlockSpec(memory_space=m) for m in (pltpu.VMEM, pltpu.SMEM, pl.ANY))
    bf, f32, dma = jnp.bfloat16, jnp.float32, pltpu.SemaphoreType.DMA
    down = latent_down.T
    attended, pool = pl.pallas_call(
        functools.partial(kernel, heads, toks),
        out_shape=[jax.ShapeDtypeStruct((toks, heads * VHEAD), bf), jax.ShapeDtypeStruct((toks, WIDTH), bf)],
        in_specs=[sm, vm, vm] + [hbm] * 7, out_specs=[vm, vm],
        scratch_shapes=[
            pltpu.VMEM((*grid, prow, WIDTH), bf), pltpu.VMEM((*grid, rows, WIDTH), bf),
            pltpu.VMEM((toks, WIDTH), bf), pltpu.VMEM((3, rows, WIDTH), bf),
            pltpu.VMEM(tokens.shape, bf), pltpu.VMEM(down.shape, bf),
            pltpu.VMEM(query_nope.shape, bf), pltpu.VMEM(query_rope.shape, bf), pltpu.VMEM(key_up.shape, bf), pltpu.VMEM(value_up.shape, bf),
            pltpu.VMEM((WIDTH, queries), bf), pltpu.VMEM((LATENT, queries), f32), pltpu.VMEM((8, queries), f32), pltpu.VMEM((8, queries), f32),
            pltpu.VMEM((2, KB, queries), f32), pltpu.VMEM((LATENT, KB), bf),
            dma((7,)), dma((6, 16)), dma((6, 16)), dma((3,)), dma((3,))],
        compiler_params=pltpu.CompilerParams(vmem_limit_bytes=63 << 20, collective_id=0, has_side_effects=True), name="latent_attention",
    )(prefix_length, table, latent_gain.reshape(1, LATENT), tokens, down, prefix_latent, query_nope, query_rope, key_up, value_up)
    return attended, pool.reshape(pages, PAGE * WIDTH)


def solution(mesh):
    placed = (P("seq", "head"), P("head", None), P(), P("seq", "head"), P("seq", "head"), P("head", None, None), P("head", None, None), P("seq", None), P(), P())
    return jax.shard_map(per_device, mesh=mesh, in_specs=placed, out_specs=(P("seq", "head"), P("seq", None)), check_vma=False)
```

time: 108 us -> 80.2 us (0.74); the launches traced: 106 us -> 80 us
  Pallas kernels: 87.3 us -> 73 us
  other arithmetic: 8.79 us -> 1.93 us
  local copies, waits for them, and re-layouts: 8.69 us -> 3.7 us
    pallas_call x2 -> x1, Pallas kernels: 87.3 us -> 73 us  [per_device(): pl.pallas_call(functools.partial(kernel, heads, toks), out_shape=[jax.Sha...]
    concatenate x1, other arithmetic: 7.1 us -> 0.74 us  [per_device(): jnp.concatenate([jnp.cos(angle), jnp.sin(angle), jnp.broadcast_to(row[:,...]
    gather x1 -> x0, local copies, waits for them, and re-layouts: 3.07 us -> none  [per_device(): new.reshape(page_table.shape[0], PAGE, WIDTH)[wanted]]
    unnamed x3 -> x1, local copies, waits for them, and re-layouts: 4.1 us -> 1.88 us
where the time goes in v2:
time: 80.2 us; the launch traced here: 80 us
  Pallas kernels  73 us (91%)
  local copies, waits for them, and re-layouts  3.7 us (5%)
  other arithmetic  1.93 us (2%)
  between operations  1.33 us (2%)
    pallas_call x1, Pallas kernels, per_device(): pl.pallas_call(functools.partial(kernel, heads, toks), out_shape=[jax.Sha...  73 us
    unnamed x1, local copies, waits for them, and re-layouts  1.88 us
    reshape x1, local copies, waits for them, and re-layouts, per_device(): return (attended, pool.reshape(pages, PAGE * WIDTH))  1.75 us

profile of v2, /device:TPU:104, one launch (start us, length us, event | category | flops | bytes accessed | tf_op | source)
XLA Modules:
  0.0 80.0 jit_solution(14401901306402140221)
XLA Ops:
  1.3 0.8 %select_reduce_fusion = s32[128]{0:T(128)S(1)} fusion(s32[256]{0:T(256)} %param.19, s32[128]{0:T(128)S(1)} %fusion.2), kind=kLoop, calls=%fused_computation | loop fusion | flops 98176 | bytes 2048 | tf_op jit(solution)/shard_map/reduce_sum | solution.py:322
  2.2 0.1 broadcast_in_dim.16
  2.3 0.3 multiply_cosine_fusion
  2.6 0.7 pad_maximum_fusion.tab_ref
  3.3 73.0 %latent_attention.1 = (bf16[128,2048]{1,0:T(8,128)(2,1)}, bf16[128,576]{1,0:T(8,128)(2,1)}) custom-call(s32[1]{0:T(128)} %copy.14.len_ref, f32[128,128]{1,0:T(8,128)} %pad_maximum_fusion.tab_ref, f32[1,512]{1,0:T(1,128)} %bitcast.5, bf16[128,1792]{1,0:T(8,128)(2,1)} %tok_hbm.1, bf16[576,1792]{1,0:T(8,128)(2,1)} %bitcast.4, bf16[64,576]{1,0:T(8,128)(2,1)} %pre_hbm.1, ...), custom_call_target="tpu_custom_call" | custom-call | tf_op jit(solution)/shard_map/latent_attention/pallas_call | solution.py:331
  76.4 1.7 %reshape.51 = bf16[8,9216]{1,0:T(8,128)(2,1)} reshape(bf16[128,576]{1,0:T(8,128)(2,1)} %get-tuple-element.5) | data formatting | bytes 294912 | tf_op jit(solution)/shard_map/reshape | solution.py:345
  78.1 1.9 %copy.15 = bf16[128,2048]{1,0:T(8,128)(2,1)} copy(bf16[128,2048]{1,0:T(8,128)(2,1)} %get-tuple-element.10) | data formatting | bytes 1048576
  (4 shorter events, 0.0 us)

commit v3 on v2

--- a/solution.py
+++ b/solution.py
@@ -8,11 +8,12 @@
 LATENT, ROPE, NOPE, VHEAD, PAGE = 512, 64, 128, 128, 16
 WIDTH = LATENT + ROPE
 HALF = ROPE // 2
+PADDED = 640
 KB = 512
 SCALE = (NOPE + ROPE) ** -0.5 * 1.4426950408889634
 NEG = -1e30
 ORDERS = (("x", "y", "z"), ("y", "z", "x"), ("z", "x", "y"))
-LANES = (pl.ds(0, 256), pl.ds(256, 256), pl.ds(512, 64))
+LANES = (pl.ds(0, 256), pl.ds(256, 256), pl.ds(512, 128))
 ALL = slice(None)
 
 
@@ -119,6 +120,51 @@
             self.copy(self.group(2, chip), slot, self.here, 1 - self.core).wait_send()
 
 
+PLANES = (("z", "x", "y"), ("x", "y", "z"))
+
+
+class Plane(Spread):
+    def __init__(self, buf, here, core, send, recv):
+        super().__init__(buf, ALL, PLANES[core], here, core, send, recv)
+
+    def near(self, i, j):
+        a, b, _ = self.order
+        return {**self.here, a: (self.here[a] + i + 4) % 4, b: (self.here[b] + j + 4) % 4}
+
+    def spots(self):
+        return [(i, j) for i in (1, 3, 0, 2) for j in (1, 3, 0, 2) if i or j]
+
+    def plane(self):
+        for i, j in self.spots():
+            self.copy(self.here, 4 * i + j, self.near(i, j), self.core).start()
+
+    def plane_landed(self):
+        for i, j in self.spots():
+            self.landed(self.near(-i, -j), 4 * i + j)
+
+    def across(self):
+        for j in (1, 3, 2):
+            self.copy(self.group(2, self.here), 15 + j, self.shifted(self.order[2], j), self.core).start()
+        self.other(self.here, 19)
+
+    def across_landed(self, k):
+        chip = self.shifted(self.order[2], k)
+        self.landed(self.group(2, chip), 15 + (4 - k) % 4)
+        self.other(chip, 19 + k)
+
+    def block_landed(self, k):
+        twin = Plane(self.buf, self.here, 1 - self.core, self.send, self.recv)
+        twin.landed(twin.group(2, twin.shifted(twin.order[2], k)), 19 + k)
+
+    def all_sent(self):
+        for i, j in self.spots():
+            self.copy(self.here, 4 * i + j, self.near(i, j), self.core).wait_send()
+        for j in (1, 2, 3):
+            self.copy(self.group(2, self.here), 15 + j, self.shifted(self.order[2], j), self.core).wait_send()
+        for k in range(4):
+            self.copy(self.group(2, self.shifted(self.order[2], k)), 19 + k, self.here, 1 - self.core).wait_send()
+
+
 def position():
     seq, head = lax.axis_index("seq"), lax.axis_index("head")
     here = {"x": seq % 4, "y": (head // 2) * 2 + seq // 16, "z": (seq // 4) % 4}
@@ -127,17 +173,33 @@
 
 def greet(here, core):
     barrier = pltpu.get_barrier_semaphore()
-    peers = [({**here, d: (here[d] + j) % 4}, core) for d in "xyz" for j in (1, 2, 3)]
-    peers += [(here, 1 - core), ({**here, "y": (here["y"] + 2) % 4}, 1 - core)]
-    for chip, c in peers:
+
+    def signal(chip, c):
         pl.semaphore_signal(barrier, inc=1, device_id=place(chip, c), device_id_type=pl.DeviceIdType.MESH)
-    pl.semaphore_wait(barrier, len(peers))
+
+    for d in "xyz":
+        for j in (1, 2, 3):
+            signal({**here, d: (here[d] + j) % 4}, core)
+    signal(here, 1 - core)
+    signal({**here, "y": (here["y"] + 2) % 4}, 1 - core)
+    for c in range(2):
+        @pl.when(core == c)
+        def _():
+            a, b, _ = PLANES[c]
+            for i in (1, 2, 3):
+                for j in (1, 2, 3):
+                    signal({**here, a: (here[a] + i) % 4, b: (here[b] + j) % 4}, c)
+
+
+def greeted():
+    pl.semaphore_wait(pltpu.get_barrier_semaphore(), 20)
 
 
 def finish(mixed, gain, cos, sin):
-    latent, a, b = mixed[:, :LATENT], mixed[:, LATENT : LATENT + HALF], mixed[:, LATENT + HALF :]
+    latent, a, b = mixed[:, :LATENT], mixed[:, LATENT : LATENT + HALF], mixed[:, LATENT + HALF : WIDTH]
     normed = latent * lax.rsqrt(jnp.mean(latent * latent, axis=1, keepdims=True) + 1e-06) * gain
-    return jnp.concatenate([normed, a * cos - b * sin, a * sin + b * cos], axis=1).astype(jnp.bfloat16)
+    spare = jnp.zeros((mixed.shape[0], PADDED - WIDTH), jnp.float32)
+    return jnp.concatenate([normed, a * cos - b * sin, a * sin + b * cos, spare], axis=1).astype(jnp.bfloat16)
 
 
 def each(group, name, *args):
@@ -146,25 +208,29 @@
 
 
 def kernel(heads, toks, len_ref, tab_ref, gain_ref, tok_hbm, down_hbm, pre_hbm, qn_hbm, qr_hbm, ku_hbm, vu_hbm,
-           out_ref, pool_ref, pbuf, nbuf, part, parts, tok_ref, down_ref, qn_ref, qr_ref, ku_ref, vu_ref,
-           qt, acc, m_s, l_s, sb, vt, in_sem, send, recv, rs_send, rs_recv):
+           out_ref, pool_ref, pbuf, nbuf, pown, part, parts, tok_ref, down_ref, qn_ref, qr_ref, ku_ref, vu_ref,
+           qt, acc, m_s, l_s, sb, vt, in_sem, pre_send, pre_recv, send, recv, rs_send, rs_recv):
     here, core, head = position()
     seq = lax.axis_index("seq")
     rows, prow = nbuf.shape[5], pbuf.shape[5]
     mine = (here["y"] % 2, here["z"], here["x"], here["y"] // 2, core)
     loads = [pltpu.make_async_copy(src, dst, in_sem.at[i]) for i, (src, dst) in enumerate((
-        (pre_hbm.at[pl.ds(head * prow, prow), :], pbuf.at[mine]), (tok_hbm, tok_ref), (down_hbm, down_ref),
+        (tok_hbm, tok_ref), (down_hbm, down_ref), (pre_hbm.at[pl.ds(head * prow, prow), :], pown),
         (qn_hbm, qn_ref), (ku_hbm, ku_ref), (qr_hbm, qr_ref), (vu_hbm, vu_ref)))]
     for load in loads:
         load.start()
     greet(here, core)
+    new = [Spread(nbuf, LANES[i], ORDERS[(i + 1) % 3], here, core, send.at[i], recv.at[i]) for i in range(3)]
+
+    def prefix(name, *args):
+        for c in range(2):
+            @pl.when(core == c)
+            def _():
+                getattr(Plane(pbuf, here, c, pre_send, pre_recv), name)(*args)
+
+
     loads[0].wait()
-    pre = [Spread(pbuf, LANES[i], ORDERS[i], here, core, send.at[i], recv.at[i]) for i in range(3)]
-    new = [Spread(nbuf, LANES[i], ORDERS[(i + 1) % 3], here, core, send.at[3 + i], recv.at[3 + i]) for i in range(3)]
-    each(pre, "ring", 0)
-
     loads[1].wait()
-    loads[2].wait()
     term = lax.dot_general(tok_ref[...], down_ref[...], (((1,), (1,)), ((), ())), preferred_element_type=jnp.float32)
     part[...] = term.astype(jnp.bfloat16)
 
@@ -174,11 +240,37 @@
             src_ref=part.at[pl.ds(to * rows, rows), :], dst_ref=parts.at[j - 1], send_sem=rs_send.at[j - 1], recv_sem=rs_recv.at[j - 1],
             device_id={"seq": seq, "head": to}, device_id_type=pl.DeviceIdType.MESH)
 
+    def lift(h):
+        cols = pl.ds(h * toks, toks)
+        lifted = jnp.dot(qn_ref[:, pl.ds(h * NOPE, NOPE)], ku_ref[h], preferred_element_type=jnp.float32)
+        qt[:LATENT, cols] = lifted.T.astype(jnp.bfloat16)
+
+    turn = tab_ref[...].T
+
+    def rotate(g):
+        cos, sin = turn[:HALF], turn[HALF : 2 * HALF]
+        both = qr_ref[:, pl.ds(g * 2 * ROPE, 2 * ROPE)].astype(jnp.float32).T
+        for e in range(2):
+            a, b = both[ROPE * e : ROPE * e + HALF], both[ROPE * e + HALF : ROPE * (e + 1)]
+            cols = pl.ds((2 * g + e) * toks, toks)
+            qt[LATENT : LATENT + HALF, cols] = (a * cos - b * sin).astype(jnp.bfloat16)
+            qt[LATENT + HALF : WIDTH, cols] = (a * sin + b * cos).astype(jnp.bfloat16)
+
+    loads[2].wait()
+    spare = (prow, PADDED - WIDTH)
+    row = seq * 4 * prow + head * prow + lax.broadcasted_iota(jnp.int32, spare, 0)
+    dead = (row >= len_ref[0]) & (lax.broadcasted_iota(jnp.int32, spare, 1) == 0)
+    pbuf[mine] = jnp.concatenate([pown[...], jnp.where(dead, NEG, 0.0).astype(jnp.bfloat16)], axis=1)
+    loads[3].wait()
+    loads[4].wait()
+    for h in range(heads // 2):
+        lift(h)
+    greeted()
     for j in (1, 2, 3):
         share(j).start()
-    each(pre, "ring_landed", 0)
-    each(pre, "ring", 1)
-    turn = tab_ref[...].T
+    prefix("plane")
+    for h in range(heads // 2, heads):
+        lift(h)
     for j in (1, 2, 3):
         share(j).wait_recv()
     own_rows = pl.ds(pl.multiple_of(head * rows, rows), rows)
@@ -187,53 +279,28 @@
         mixed += parts[j].astype(jnp.float32)
     nbuf[mine] = finish(mixed, gain_ref[...], tab_ref[own_rows, :HALF], tab_ref[own_rows, HALF : 2 * HALF])
     each(new, "ring", 0)
-
-    def lift(h):
-        cols = pl.ds(h * toks, toks)
-        lifted = jnp.dot(qn_ref[:, pl.ds(h * NOPE, NOPE)], ku_ref[h], preferred_element_type=jnp.float32)
-        qt[:LATENT, cols] = lifted.T.astype(jnp.bfloat16)
-
-    def rotate(g):
-        cos, sin = turn[:HALF], turn[HALF : 2 * HALF]
-        both = qr_ref[:, pl.ds(g * 2 * ROPE, 2 * ROPE)].astype(jnp.float32).T
-        for e in range(2):
-            a, b = both[ROPE * e : ROPE * e + HALF], both[ROPE * e + HALF : ROPE * (e + 1)]
-            cols = pl.ds((2 * g + e) * toks, toks)
-            qt[LATENT : LATENT + HALF, cols] = (a * cos - b * sin).astype(jnp.bfloat16)
-            qt[LATENT + HALF :, cols] = (a * sin + b * cos).astype(jnp.bfloat16)
-
-    loads[3].wait()
-    loads[4].wait()
-    for h in range(heads // 2):
-        lift(h)
-    each(pre, "ring_landed", 1)
-    each(pre, "last")
-    each(new, "ring_landed", 0)
-    each(new, "ring", 1)
-    for h in range(heads // 2, heads):
-        lift(h)
+    prefix("plane_landed")
+    prefix("across")
     loads[5].wait()
-    each(pre, "forward")
     for g in range(heads // 2):
         rotate(g)
+    ones = lax.broadcasted_iota(jnp.int32, (PADDED - WIDTH, heads * toks), 0) == 0
+    qt[WIDTH:, :] = jnp.where(ones, 1.0, 0.0).astype(jnp.bfloat16)
     m_s[...] = jnp.full_like(m_s, NEG)
     l_s[...] = jnp.zeros_like(l_s)
     acc[...] = jnp.zeros_like(acc)
-    each(new, "ring_landed", 1)
-    each(new, "last")
-    each(pre, "sides")
-    each(pre, "far")
-    each(pre, "others_landed")
 
     first_row = seq * toks
     own_blocks = (first_row + toks + KB - 1) // KB
-    pre_blocks = pbuf.size // (WIDTH * KB)
-
-    def pre_keys(b):
-        return pbuf[b // 2, pl.ds(2 * (b % 2), 2)].reshape(KB, WIDTH)
+
+    def pre_keys(k):
+        y, z = (here["y"] + k) % 4, (here["z"] + k) % 4
+        even = pbuf[y % 2, :, :, y // 2, 0].reshape(KB // 2, PADDED)
+        odd = pbuf[:, z, :, :, 1].reshape(KB // 2, PADDED)
+        return jnp.concatenate([even, odd], axis=0)
 
     def new_keys(b):
-        return nbuf[b // 4, b % 4].reshape(KB, WIDTH)
+        return nbuf[b // 4, b % 4].reshape(KB, PADDED)
 
     def score(keys, slot):
         sb[slot] = jnp.dot(keys, qt[...], preferred_element_type=jnp.float32)
@@ -251,10 +318,9 @@
         def _():
             hide(slot, first_row - b * KB, 1)
 
-    def score_pre(b, slot):
-        score(pre_keys(b), slot)
-        if b >= 2:
-            hide(slot, len_ref[0] - b * KB - 1, 0)
+    def score_pre(k, slot):
+        prefix("block_landed", k)
+        score(pre_keys(k), slot)
 
     def soft(keys, slot):
         vt[...] = keys[:, :LATENT].T
@@ -268,18 +334,25 @@
         acc[...] = acc[...] * fade + jnp.dot(vt[...], w.astype(jnp.bfloat16), preferred_element_type=jnp.float32)
 
     score_pre(0, 0)
+    each(new, "ring_landed", 0)
+    each(new, "ring", 1)
+    prefix("across_landed", 1)
+    prefix("across_landed", 3)
     score_pre(1, 1)
     soft(pre_keys(0), 0)
+    each(new, "ring_landed", 1)
+    each(new, "last")
+    prefix("across_landed", 2)
+    score_pre(3, 0)
+    soft(pre_keys(1), 1)
     each(new, "forward")
-    score_pre(2, 0)
-    soft(pre_keys(1), 1)
+    score_pre(2, 1)
+    soft(pre_keys(3), 0)
     each(new, "sides")
-    score_pre(3, 1)
-    soft(pre_keys(2), 0)
     each(new, "far")
     each(new, "others_landed")
     score_new(0, 0)
-    soft(pre_keys(3), 1)
+    soft(pre_keys(2), 1)
 
     def step(pair, carry):
         for u in range(2):
@@ -294,17 +367,17 @@
 
     wanted = tab_ref[:, 2 * HALF : 2 * HALF + 1]
     picked = jnp.zeros((toks, WIDTH), jnp.float32)
-    for b in range(nbuf.size // (WIDTH * KB)):
+    for b in range(nbuf.size // (PADDED * KB)):
         row = lax.broadcasted_iota(jnp.int32, (toks, KB), 1).astype(jnp.float32) + float(b * KB)
         pick = jnp.where(row == wanted, 1.0, 0.0).astype(jnp.bfloat16)
-        picked += jnp.dot(pick, new_keys(b), preferred_element_type=jnp.float32)
+        picked += jnp.dot(pick, new_keys(b)[:, :WIDTH], preferred_element_type=jnp.float32)
     pool_ref[...] = picked.astype(jnp.bfloat16)
     loads[6].wait()
     for h in range(heads):
         cols = pl.ds(h * toks, toks)
         att = (acc[:, cols] / l_s[0:1, cols]).astype(jnp.bfloat16)
         out_ref[:, pl.ds(h * VHEAD, VHEAD)] = lax.dot_general(att, vu_ref[h], (((0,), (0,)), ((), ())), preferred_element_type=jnp.float32).astype(jnp.bfloat16)
-    each(pre, "sent")
+    prefix("all_sent")
     each(new, "sent")
     for j in (1, 2, 3):
         share(j).wait_send()
@@ -333,13 +406,13 @@
         out_shape=[jax.ShapeDtypeStruct((toks, heads * VHEAD), bf), jax.ShapeDtypeStruct((toks, WIDTH), bf)],
         in_specs=[sm, vm, vm] + [hbm] * 7, out_specs=[vm, vm],
         scratch_shapes=[
-            pltpu.VMEM((*grid, prow, WIDTH), bf), pltpu.VMEM((*grid, rows, WIDTH), bf),
-            pltpu.VMEM((toks, WIDTH), bf), pltpu.VMEM((3, rows, WIDTH), bf),
+            pltpu.VMEM((*grid, prow, PADDED), bf), pltpu.VMEM((*grid, rows, PADDED), bf),
+            pltpu.VMEM((prow, WIDTH), bf), pltpu.VMEM((toks, WIDTH), bf), pltpu.VMEM((3, rows, WIDTH), bf),
             pltpu.VMEM(tokens.shape, bf), pltpu.VMEM(down.shape, bf),
             pltpu.VMEM(query_nope.shape, bf), pltpu.VMEM(query_rope.shape, bf), pltpu.VMEM(key_up.shape, bf), pltpu.VMEM(value_up.shape, bf),
-            pltpu.VMEM((WIDTH, queries), bf), pltpu.VMEM((LATENT, queries), f32), pltpu.VMEM((8, queries), f32), pltpu.VMEM((8, queries), f32),
+            pltpu.VMEM((PADDED, queries), bf), pltpu.VMEM((LATENT, queries), f32), pltpu.VMEM((8, queries), f32), pltpu.VMEM((8, queries), f32),
             pltpu.VMEM((2, KB, queries), f32), pltpu.VMEM((LATENT, KB), bf),
-            dma((7,)), dma((6, 16)), dma((6, 16)), dma((3,)), dma((3,))],
+            dma((7,)), dma((23,)), dma((23,)), dma((3, 16)), dma((3, 16)), dma((3,)), dma((3,))],
         compiler_params=pltpu.CompilerParams(vmem_limit_bytes=63 << 20, collective_id=0, has_side_effects=True), name="latent_attention",
     )(prefix_length, table, latent_gain.reshape(1, LATENT), tokens, down, prefix_latent, query_nope, query_rope, key_up, value_up)
     return attended, pool.reshape(pages, PAGE * WIDTH)

time: 80.2 us -> 80 us (level); the launches traced: 80 us -> 78.4 us
  Pallas kernels: 73 us -> 71.5 us
    pallas_call x1, Pallas kernels: 73 us -> 71.5 us  [per_device(): pl.pallas_call(functools.partial(kernel, heads, toks), out_shape=[jax.Sha...]
where the time goes in v3:
time: 80 us; the launch traced here: 78.4 us
  Pallas kernels  71.5 us (89%)
  local copies, waits for them, and re-layouts  3.7 us (5%)
  other arithmetic  1.93 us (2%)
  between operations  1.33 us (2%)
    pallas_call x1, Pallas kernels, per_device(): pl.pallas_call(functools.partial(kernel, heads, toks), out_shape=[jax.Sha...  71.5 us
    unnamed x1, local copies, waits for them, and re-layouts  1.88 us
    reshape x1, local copies, waits for them, and re-layouts, per_device(): return (attended, pool.reshape(pages, PAGE * WIDTH))  1.75 us

profile of v3, /device:TPU:104, one launch (start us, length us, event | category | flops | bytes accessed | tf_op | source)
XLA Modules:
  0.0 78.4 jit_solution(13430846433952795203)
XLA Ops:
  1.3 0.8 %select_reduce_fusion = s32[128]{0:T(128)S(1)} fusion(s32[256]{0:T(256)} %param.19, s32[128]{0:T(128)S(1)} %fusion.2), kind=kLoop, calls=%fused_computation | loop fusion | flops 98176 | bytes 2048 | tf_op jit(solution)/shard_map/reduce_sum | solution.py:395
  2.2 0.1 broadcast_in_dim.16
  2.3 0.3 multiply_cosine_fusion
  2.6 0.7 pad_maximum_fusion.tab_ref
  3.3 71.5 %latent_attention.1 = (bf16[128,2048]{1,0:T(8,128)(2,1)}, bf16[128,576]{1,0:T(8,128)(2,1)}) custom-call(s32[1]{0:T(128)} %copy.14.len_ref, f32[128,128]{1,0:T(8,128)} %pad_maximum_fusion.tab_ref, f32[1,512]{1,0:T(1,128)} %bitcast.5, bf16[128,1792]{1,0:T(8,128)(2,1)} %tok_hbm.1, bf16[576,1792]{1,0:T(8,128)(2,1)} %bitcast.4, bf16[64,576]{1,0:T(8,128)(2,1)} %pre_hbm.1, ...), custom_call_target="tpu_custom_call" | custom-call | tf_op jit(solution)/shard_map/latent_attention/pallas_call | solution.py:404
  74.8 1.7 %reshape.51 = bf16[8,9216]{1,0:T(8,128)(2,1)} reshape(bf16[128,576]{1,0:T(8,128)(2,1)} %get-tuple-element.5) | data formatting | bytes 294912 | tf_op jit(solution)/shard_map/reshape | solution.py:418
  76.6 1.9 %copy.15 = bf16[128,2048]{1,0:T(8,128)(2,1)} copy(bf16[128,2048]{1,0:T(8,128)(2,1)} %get-tuple-element.10) | data formatting | bytes 1048576
  (4 shorter events, 0.0 us)

commit v4 on v3

--- a/solution.py
+++ b/solution.py
@@ -12,8 +12,6 @@
 KB = 512
 SCALE = (NOPE + ROPE) ** -0.5 * 1.4426950408889634
 NEG = -1e30
-ORDERS = (("x", "y", "z"), ("y", "z", "x"), ("z", "x", "y"))
-LANES = (pl.ds(0, 256), pl.ds(256, 256), pl.ds(512, 128))
 ALL = slice(None)
 
 
@@ -29,6 +27,8 @@
 
 
 class Spread:
+    cross = 5
+
     def __init__(self, buf, lanes, order, here, core, send, recv):
         self.buf, self.lanes, self.order = buf, lanes, order
         self.here, self.core, self.send, self.recv = here, core, send, recv
@@ -51,10 +51,6 @@
     def group(self, depth, chip):
         return {**chip, **{d: ALL for d in self.order[:depth]}}
 
-    def half(self, chip, k):
-        dim = [d for d in self.order[:2] if d != "y"][0]
-        return {**self.group(2, chip), dim: pl.ds(2 * k, 2)}
-
     def ring(self, depth):
         dim = self.order[depth]
         for j in (1, 3, 2):
@@ -65,67 +61,50 @@
         for j in (1, 3, 2):
             self.landed(self.group(depth, self.shifted(dim, -j)), 3 * depth + j - 1)
 
-    def last(self):
-        dim = self.order[2]
-        right, left = self.shifted(dim, 1), self.shifted(dim, -1)
-        self.copy(self.half(self.here, 0), 6, right, self.core).start()
-        self.copy(self.half(self.here, 1), 7, left, self.core).start()
-        self.copy(self.half(self.here, 1), 8, right, self.core).start()
-        self.copy(self.half(self.here, 0), 9, left, self.core).start()
-        self.other(self.here, 12)
-
     def other(self, chip, slot):
         self.copy(self.group(2, chip), slot, self.here, 1 - self.core).start()
 
-    def forward(self):
-        dim = self.order[2]
-        right, left = self.shifted(dim, 1), self.shifted(dim, -1)
-        self.landed(self.half(left, 0), 6)
-        self.copy(self.half(left, 0), 10, right, self.core).start()
-        self.landed(self.half(right, 1), 7)
-        self.copy(self.half(right, 1), 11, left, self.core).start()
-
-    def sides(self):
-        dim = self.order[2]
-        right, left = self.shifted(dim, 1), self.shifted(dim, -1)
-        self.landed(self.half(left, 1), 8)
-        self.other(left, 13)
-        self.landed(self.half(right, 0), 9)
-        self.other(right, 14)
-
-    def far(self):
-        far = self.shifted(self.order[2], 2)
-        self.landed(self.half(far, 0), 10)
-        self.landed(self.half(far, 1), 11)
-        self.other(far, 15)
-
-    def others_landed(self):
-        dim = self.order[2]
-        for j, slot in ((0, 12), (-1, 13), (1, 14), (2, 15)):
-            chip = self.group(2, self.shifted(dim, j))
-            ref = view(self.buf, chip, 1 - self.core, self.lanes)
-            pltpu.make_async_remote_copy(
-                src_ref=ref, dst_ref=ref, send_sem=self.send.at[slot], recv_sem=self.recv.at[slot],
-                device_id=place(self.here, 1 - self.core), device_id_type=pl.DeviceIdType.MESH).wait_recv()
-
-    def sent(self):
-        dim = self.order[2]
-        right, left, far = self.shifted(dim, 1), self.shifted(dim, -1), self.shifted(dim, 2)
+    def across(self):
+        for j in (1, 3, 2):
+            self.copy(self.group(2, self.here), self.cross + j, self.shifted(self.order[2], j), self.core).start()
+        self.other(self.here, self.cross + 4)
+
+    def across_landed(self, k):
+        chip = self.shifted(self.order[2], k)
+        self.landed(self.group(2, chip), self.cross + (4 - k) % 4)
+        self.other(chip, self.cross + 4 + k)
+
+    def twin(self):
+        return Spread(self.buf, self.lanes, self.order, self.here, 1 - self.core, self.send, self.recv)
+
+    def block_landed(self, k):
+        twin = self.twin()
+        twin.landed(twin.group(2, twin.shifted(twin.order[2], k)), self.cross + 4 + k)
+
+    def near_sent(self):
         for depth in (0, 1):
             for j in (1, 2, 3):
                 self.copy(self.group(depth, self.here), 3 * depth + j - 1, self.shifted(self.order[depth], j), self.core).wait_send()
-        for slot, chip, k, to in ((6, self.here, 0, right), (7, self.here, 1, left), (8, self.here, 1, right), (9, self.here, 0, left), (10, left, 0, right), (11, right, 1, left)):
-            self.copy(self.half(chip, k), slot, to, self.core).wait_send()
-        for slot, chip in ((12, self.here), (13, left), (14, right), (15, far)):
-            self.copy(self.group(2, chip), slot, self.here, 1 - self.core).wait_send()
+
+    def all_sent(self):
+        self.near_sent()
+        for j in (1, 2, 3):
+            self.copy(self.group(2, self.here), self.cross + j, self.shifted(self.order[2], j), self.core).wait_send()
+        for k in range(4):
+            self.copy(self.group(2, self.shifted(self.order[2], k)), self.cross + 4 + k, self.here, 1 - self.core).wait_send()
 
 
 PLANES = (("z", "x", "y"), ("x", "y", "z"))
 
 
 class Plane(Spread):
+    cross = 15
+
     def __init__(self, buf, here, core, send, recv):
         super().__init__(buf, ALL, PLANES[core], here, core, send, recv)
+
+    def twin(self):
+        return Plane(self.buf, self.here, 1 - self.core, self.send, self.recv)
 
     def near(self, i, j):
         a, b, _ = self.order
@@ -142,27 +121,9 @@
         for i, j in self.spots():
             self.landed(self.near(-i, -j), 4 * i + j)
 
-    def across(self):
-        for j in (1, 3, 2):
-            self.copy(self.group(2, self.here), 15 + j, self.shifted(self.order[2], j), self.core).start()
-        self.other(self.here, 19)
-
-    def across_landed(self, k):
-        chip = self.shifted(self.order[2], k)
-        self.landed(self.group(2, chip), 15 + (4 - k) % 4)
-        self.other(chip, 19 + k)
-
-    def block_landed(self, k):
-        twin = Plane(self.buf, self.here, 1 - self.core, self.send, self.recv)
-        twin.landed(twin.group(2, twin.shifted(twin.order[2], k)), 19 + k)
-
-    def all_sent(self):
+    def near_sent(self):
         for i, j in self.spots():
             self.copy(self.here, 4 * i + j, self.near(i, j), self.core).wait_send()
-        for j in (1, 2, 3):
-            self.copy(self.group(2, self.here), 15 + j, self.shifted(self.order[2], j), self.core).wait_send()
-        for k in range(4):
-            self.copy(self.group(2, self.shifted(self.order[2], k)), 19 + k, self.here, 1 - self.core).wait_send()
 
 
 def position():
@@ -200,11 +161,6 @@
     normed = latent * lax.rsqrt(jnp.mean(latent * latent, axis=1, keepdims=True) + 1e-06) * gain
     spare = jnp.zeros((mixed.shape[0], PADDED - WIDTH), jnp.float32)
     return jnp.concatenate([normed, a * cos - b * sin, a * sin + b * cos, spare], axis=1).astype(jnp.bfloat16)
-
-
-def each(group, name, *args):
-    for item in group:
-        getattr(item, name)(*args)
 
 
 def kernel(heads, toks, len_ref, tab_ref, gain_ref, tok_hbm, down_hbm, pre_hbm, qn_hbm, qr_hbm, ku_hbm, vu_hbm,
@@ -220,19 +176,21 @@
     for load in loads:
         load.start()
     greet(here, core)
-    new = [Spread(nbuf, LANES[i], ORDERS[(i + 1) % 3], here, core, send.at[i], recv.at[i]) for i in range(3)]
-
-    def prefix(name, *args):
-        for c in range(2):
-            @pl.when(core == c)
-            def _():
-                getattr(Plane(pbuf, here, c, pre_send, pre_recv), name)(*args)
-
+    def planes(buf, sends, recvs):
+        def run(name, *args):
+            for c in range(2):
+                @pl.when(core == c)
+                def _():
+                    getattr(Plane(buf, here, c, sends, recvs), name)(*args)
+        return run
+
+    prefix, new = planes(pbuf, pre_send, pre_recv), planes(nbuf, send, recv)
 
     loads[0].wait()
     loads[1].wait()
     term = lax.dot_general(tok_ref[...], down_ref[...], (((1,), (1,)), ((), ())), preferred_element_type=jnp.float32)
-    part[...] = term.astype(jnp.bfloat16)
+    part[:, :WIDTH] = term.astype(jnp.bfloat16)
+    part[:, WIDTH:] = jnp.zeros((part.shape[0], PADDED - WIDTH), jnp.bfloat16)
 
     def share(j):
         to = (head + j) % 4
@@ -278,7 +236,7 @@
     for j in range(3):
         mixed += parts[j].astype(jnp.float32)
     nbuf[mine] = finish(mixed, gain_ref[...], tab_ref[own_rows, :HALF], tab_ref[own_rows, HALF : 2 * HALF])
-    each(new, "ring", 0)
+    new("plane")
     prefix("plane_landed")
     prefix("across")
     loads[5].wait()
@@ -291,7 +249,6 @@
     acc[...] = jnp.zeros_like(acc)
 
     first_row = seq * toks
-    own_blocks = (first_row + toks + KB - 1) // KB
 
     def pre_keys(k):
         y, z = (here["y"] + k) % 4, (here["z"] + k) % 4
@@ -299,24 +256,36 @@
         odd = pbuf[:, z, :, :, 1].reshape(KB // 2, PADDED)
         return jnp.concatenate([even, odd], axis=0)
 
-    def new_keys(b):
-        return nbuf[b // 4, b % 4].reshape(KB, PADDED)
+    def new_keys(k, odd):
+        y, z = (here["y"] + k) % 4, (here["z"] + k) % 4
+        if odd:
+            return nbuf[:, z, :, :, 1].reshape(KB, PADDED)
+        return nbuf[y % 2, :, :, y // 2, 0].reshape(KB, PADDED)
+
+    def place_of(k, odd):
+        y, z = (here["y"] + k) % 4, (here["z"] + k) % 4
+        m = lax.broadcasted_iota(jnp.int32, (KB, toks), 0)
+        r, x = m % rows, m // (2 * rows if odd else rows) % 4
+        if odd:
+            s, h = m // (8 * rows) * 16 + z * 4 + x, m // rows % 2 * 2 + 1
+            last = (19 + z * 4) * toks + toks - 1
+        else:
+            s, h = y % 2 * 16 + m // (4 * rows) * 4 + x, y // 2 * 2
+            last = (y % 2 * 16 + 15) * toks + toks - 1
+        return s * toks + h * rows + r, last
 
     def score(keys, slot):
         sb[slot] = jnp.dot(keys, qt[...], preferred_element_type=jnp.float32)
 
-    def hide(slot, limit, step):
-        for h in range(heads):
-            cols = pl.ds(h * toks, toks)
-            key = lax.broadcasted_iota(jnp.int32, (KB, toks), 0)
-            tok = lax.broadcasted_iota(jnp.int32, (KB, toks), 1)
-            sb[slot, :, cols] = jnp.where(key <= tok * step + limit, sb[slot, :, cols], NEG)
-
-    def score_new(b, slot):
-        score(new_keys(b), slot)
-        @pl.when(b == own_blocks - 1)
+    def hide(k, odd):
+        row, last = place_of(k, odd)
+
+        @pl.when(last > first_row)
         def _():
-            hide(slot, first_row - b * KB, 1)
+            live = row <= first_row + lax.broadcasted_iota(jnp.int32, (KB, toks), 1)
+            for h in range(heads):
+                cols = pl.ds(h * toks, toks)
+                sb[odd, :, cols] = jnp.where(live, sb[odd, :, cols], NEG)
 
     def score_pre(k, slot):
         prefix("block_landed", k)
@@ -334,53 +303,74 @@
         acc[...] = acc[...] * fade + jnp.dot(vt[...], w.astype(jnp.bfloat16), preferred_element_type=jnp.float32)
 
     score_pre(0, 0)
-    each(new, "ring_landed", 0)
-    each(new, "ring", 1)
+    new("plane_landed")
+    new("across")
+    soft(pre_keys(0), 0)
     prefix("across_landed", 1)
     prefix("across_landed", 3)
     score_pre(1, 1)
-    soft(pre_keys(0), 0)
-    each(new, "ring_landed", 1)
-    each(new, "last")
     prefix("across_landed", 2)
-    score_pre(3, 0)
+    prefix("block_landed", 3)
+    score(pre_keys(3), 0)
     soft(pre_keys(1), 1)
-    each(new, "forward")
-    score_pre(2, 1)
+    prefix("block_landed", 2)
+    score(pre_keys(2), 1)
     soft(pre_keys(3), 0)
-    each(new, "sides")
-    each(new, "far")
-    each(new, "others_landed")
-    score_new(0, 0)
+    new("block_landed", 0)
+    score(new_keys(0, 0), 0)
     soft(pre_keys(2), 1)
-
-    def step(pair, carry):
-        for u in range(2):
-            b = pair * 2 + u
-            @pl.when(b < own_blocks)
-            def _():
-                score_new(jnp.minimum(b + 1, own_blocks - 1), 1 - u)
-                soft(new_keys(b), u)
+    hide(0, 0)
+
+    def step(i, carry):
+        k, k_next = i + i // 2 - i // 3 * 2, i + 1 + (i + 1) // 2 - (i + 1) // 3 * 2
+
+        @pl.when(i < 3)
+        def _():
+            new("across_landed", k_next)
+
+        score(new_keys(k, 1), 1)
+        soft(new_keys(k, 0), 0)
+        hide(k, 1)
+
+        @pl.when(i < 3)
+        def _():
+            new("block_landed", k_next)
+            score(new_keys(k_next, 0), 0)
+            soft(new_keys(k, 1), 1)
+            hide(k_next, 0)
+
+        @pl.when(i == 3)
+        def _():
+            soft(new_keys(k, 1), 1)
         return carry
 
-    lax.fori_loop(0, (own_blocks + 1) // 2, step, 0)
+    lax.fori_loop(0, 4, step, 0)
 
     wanted = tab_ref[:, 2 * HALF : 2 * HALF + 1]
     picked = jnp.zeros((toks, WIDTH), jnp.float32)
-    for b in range(nbuf.size // (PADDED * KB)):
+    for b in range(8):
         row = lax.broadcasted_iota(jnp.int32, (toks, KB), 1).astype(jnp.float32) + float(b * KB)
         pick = jnp.where(row == wanted, 1.0, 0.0).astype(jnp.bfloat16)
-        picked += jnp.dot(pick, new_keys(b)[:, :WIDTH], preferred_element_type=jnp.float32)
-    pool_ref[...] = picked.astype(jnp.bfloat16)
+        keys = nbuf[b // 4, b % 4].reshape(KB, PADDED)
+        picked += jnp.dot(pick, keys[:, :WIDTH], preferred_element_type=jnp.float32)
+    pool_ref[...] = picked
     loads[6].wait()
     for h in range(heads):
         cols = pl.ds(h * toks, toks)
         att = (acc[:, cols] / l_s[0:1, cols]).astype(jnp.bfloat16)
         out_ref[:, pl.ds(h * VHEAD, VHEAD)] = lax.dot_general(att, vu_ref[h], (((0,), (0,)), ((), ())), preferred_element_type=jnp.float32).astype(jnp.bfloat16)
     prefix("all_sent")
-    each(new, "sent")
+    new("all_sent")
     for j in (1, 2, 3):
         share(j).wait_send()
+
+
+def leave(att_ref, rows_ref, out_ref, pool_ref):
+    out_ref[...] = att_ref[...]
+    pages = pool_ref.shape[0]
+    for r in range(0, PAGE, 2):
+        pair = [rows_ref[pl.ds((r + e) * pages, pages), :] for e in range(2)]
+        pool_ref[:, pl.ds(r * WIDTH, 2 * WIDTH)] = jnp.concatenate(pair, axis=1).astype(jnp.bfloat16)
 
 
 def per_device(tokens, latent_down, latent_gain, query_nope, query_rope, key_up, value_up, prefix_latent, prefix_length, page_table):
@@ -390,10 +380,10 @@
     frequency = 10000.0 ** (-jnp.arange(HALF, dtype=jnp.float32) / HALF)
     angle = positions.astype(jnp.float32)[:, None] * frequency[None, :]
     pages = toks // PAGE
-    slots = seq * pages + jnp.arange(toks, dtype=jnp.int32) // PAGE
+    slots = seq * pages + jnp.arange(toks, dtype=jnp.int32) % pages
     count = page_table.shape[0]
     page = jnp.sum(jnp.where(page_table[None, :] == slots[:, None], jnp.arange(count, dtype=jnp.int32)[None, :], 0), axis=1)
-    row = (page * PAGE + jnp.arange(toks, dtype=jnp.int32) % PAGE).astype(jnp.float32)
+    row = (page * PAGE + jnp.arange(toks, dtype=jnp.int32) // pages).astype(jnp.float32)
     table = jnp.concatenate([jnp.cos(angle), jnp.sin(angle), jnp.broadcast_to(row[:, None], (toks, 2 * HALF))], axis=1)
     rows, prow = toks // 4, prefix_latent.shape[0] // 4
     grid = (2, 4, 4, 2, 2)
@@ -403,19 +393,22 @@
     down = latent_down.T
     attended, pool = pl.pallas_call(
         functools.partial(kernel, heads, toks),
-        out_shape=[jax.ShapeDtypeStruct((toks, heads * VHEAD), bf), jax.ShapeDtypeStruct((toks, WIDTH), bf)],
+        out_shape=[jax.ShapeDtypeStruct((toks, heads * VHEAD), bf), jax.ShapeDtypeStruct((toks, WIDTH), f32)],
         in_specs=[sm, vm, vm] + [hbm] * 7, out_specs=[vm, vm],
         scratch_shapes=[
             pltpu.VMEM((*grid, prow, PADDED), bf), pltpu.VMEM((*grid, rows, PADDED), bf),
-            pltpu.VMEM((prow, WIDTH), bf), pltpu.VMEM((toks, WIDTH), bf), pltpu.VMEM((3, rows, WIDTH), bf),
+            pltpu.VMEM((prow, WIDTH), bf), pltpu.VMEM((toks, PADDED), bf), pltpu.VMEM((3, rows, PADDED), bf),
             pltpu.VMEM(tokens.shape, bf), pltpu.VMEM(down.shape, bf),
             pltpu.VMEM(query_nope.shape, bf), pltpu.VMEM(query_rope.shape, bf), pltpu.VMEM(key_up.shape, bf), pltpu.VMEM(value_up.shape, bf),
             pltpu.VMEM((PADDED, queries), bf), pltpu.VMEM((LATENT, queries), f32), pltpu.VMEM((8, queries), f32), pltpu.VMEM((8, queries), f32),
             pltpu.VMEM((2, KB, queries), f32), pltpu.VMEM((LATENT, KB), bf),
-            dma((7,)), dma((23,)), dma((23,)), dma((3, 16)), dma((3, 16)), dma((3,)), dma((3,))],
+            dma((7,)), dma((23,)), dma((23,)), dma((23,)), dma((23,)), dma((3,)), dma((3,))],
         compiler_params=pltpu.CompilerParams(vmem_limit_bytes=63 << 20, collective_id=0, has_side_effects=True), name="latent_attention",
     )(prefix_length, table, latent_gain.reshape(1, LATENT), tokens, down, prefix_latent, query_nope, query_rope, key_up, value_up)
-    return attended, pool.reshape(pages, PAGE * WIDTH)
+    return tuple(pl.pallas_call(
+        leave, out_shape=[jax.ShapeDtypeStruct(attended.shape, bf), jax.ShapeDtypeStruct((pages, PAGE * WIDTH), bf)],
+        in_specs=[vm, vm], out_specs=[vm, vm], name="leave",
+    )(attended, pool))
 
 
 def solution(mesh):

time: 80 us -> 81.5 us (1.019)
  the two profiles are of different devices: /device:TPU:104 before, /device:TPU:1 now
where the time goes in v4:
time: 81.5 us; the launch traced here: 81.3 us
  Pallas kernels  77.9 us (96%)
  other arithmetic  1.93 us (2%)
  between operations  1.33 us (2%)
    pallas_call x1, Pallas kernels, per_device(): pl.pallas_call(functools.partial(kernel, heads, toks), out_shape=[jax.Sha...  75.9 us
    pallas_call x1, Pallas kernels, per_device(): pl.pallas_call(leave, out_shape=[jax.ShapeDtypeStruct(attended.shape, bf)...  2.01 us

profile of v4, /device:TPU:1, one launch (start us, length us, event | category | flops | bytes accessed | tf_op | source)
XLA Modules:
  0.0 81.3 jit_solution(5558904081871970934)
XLA Ops:
  1.3 0.8 %select_reduce_fusion = s32[128]{0:T(128)S(1)} fusion(s32[256]{0:T(256)} %param.19, s32[128]{0:T(128)S(1)} %fusion.1), kind=kLoop, calls=%fused_computation | loop fusion | flops 98176 | bytes 2048 | tf_op jit(solution)/shard_map/reduce_sum | solution.py:385
  2.2 0.1 broadcast_in_dim.16
  2.3 0.3 multiply_cosine_fusion
  2.6 0.7 pad_maximum_fusion.tab_ref
  3.3 75.9 %latent_attention.1 = (bf16[128,2048]{1,0:T(8,128)(2,1)}, f32[128,576]{1,0:T(8,128)}) custom-call(s32[1]{0:T(128)} %copy.13.len_ref, f32[128,128]{1,0:T(8,128)} %pad_maximum_fusion.tab_ref, f32[1,512]{1,0:T(1,128)} %bitcast.5, bf16[128,1792]{1,0:T(8,128)(2,1)} %tok_hbm.1, bf16[576,1792]{1,0:T(8,128)(2,1)} %bitcast.4, bf16[64,576]{1,0:T(8,128)(2,1)} %pre_hbm.1, ...), custom_call_target="tpu_custom_call" | custom-call | tf_op jit(solution)/shard_map/latent_attention/pallas_call | solution.py:394
  79.3 2.0 %leave.1 = (bf16[128,2048]{1,0:T(8,128)(2,1)}, bf16[8,9216]{1,0:T(8,128)(2,1)}) custom-call(bf16[128,2048]{1,0:T(8,128)(2,1)} %get-tuple-element.4.att_ref, f32[128,576]{1,0:T(8,128)} %get-tuple-element.5.rows_ref), custom_call_target="tpu_custom_call" | custom-call | tf_op jit(solution)/shard_map/leave/pallas_call | solution.py:408
  (4 shorter events, 0.0 us)

commit v5 on v4

--- a/solution.py
+++ b/solution.py
@@ -156,10 +156,11 @@
     pl.semaphore_wait(pltpu.get_barrier_semaphore(), 20)
 
 
-def finish(mixed, gain, cos, sin):
+def finish(mixed, gain, cos, sin, seq):
     latent, a, b = mixed[:, :LATENT], mixed[:, LATENT : LATENT + HALF], mixed[:, LATENT + HALF : WIDTH]
     normed = latent * lax.rsqrt(jnp.mean(latent * latent, axis=1, keepdims=True) + 1e-06) * gain
-    spare = jnp.zeros((mixed.shape[0], PADDED - WIDTH), jnp.float32)
+    column = lax.broadcasted_iota(jnp.int32, (mixed.shape[0], PADDED - WIDTH), 1)
+    spare = jnp.where(column == 1 + seq, 1.0, 0.0)
     return jnp.concatenate([normed, a * cos - b * sin, a * sin + b * cos, spare], axis=1).astype(jnp.bfloat16)
 
 
@@ -235,20 +236,20 @@
     mixed = part[own_rows, :].astype(jnp.float32)
     for j in range(3):
         mixed += parts[j].astype(jnp.float32)
-    nbuf[mine] = finish(mixed, gain_ref[...], tab_ref[own_rows, :HALF], tab_ref[own_rows, HALF : 2 * HALF])
+    nbuf[mine] = finish(mixed, gain_ref[...], tab_ref[own_rows, :HALF], tab_ref[own_rows, HALF : 2 * HALF], seq)
     new("plane")
     prefix("plane_landed")
     prefix("across")
     loads[5].wait()
     for g in range(heads // 2):
         rotate(g)
-    ones = lax.broadcasted_iota(jnp.int32, (PADDED - WIDTH, heads * toks), 0) == 0
-    qt[WIDTH:, :] = jnp.where(ones, 1.0, 0.0).astype(jnp.bfloat16)
+    spare_row = lax.broadcasted_iota(jnp.int32, (PADDED - WIDTH, heads * toks), 0)
+    late = (spare_row > 1 + seq) & (spare_row < 33)
+    qt[WIDTH:, :] = jnp.where(spare_row == 0, 1.0, jnp.where(late, NEG, 0.0)).astype(jnp.bfloat16)
     m_s[...] = jnp.full_like(m_s, NEG)
     l_s[...] = jnp.zeros_like(l_s)
     acc[...] = jnp.zeros_like(acc)
 
-    first_row = seq * toks
 
     def pre_keys(k):
         y, z = (here["y"] + k) % 4, (here["z"] + k) % 4
@@ -262,30 +263,19 @@
             return nbuf[:, z, :, :, 1].reshape(KB, PADDED)
         return nbuf[y % 2, :, :, y // 2, 0].reshape(KB, PADDED)
 
-    def place_of(k, odd):
-        y, z = (here["y"] + k) % 4, (here["z"] + k) % 4
-        m = lax.broadcasted_iota(jnp.int32, (KB, toks), 0)
-        r, x = m % rows, m // (2 * rows if odd else rows) % 4
-        if odd:
-            s, h = m // (8 * rows) * 16 + z * 4 + x, m // rows % 2 * 2 + 1
-            last = (19 + z * 4) * toks + toks - 1
-        else:
-            s, h = y % 2 * 16 + m // (4 * rows) * 4 + x, y // 2 * 2
-            last = (y % 2 * 16 + 15) * toks + toks - 1
-        return s * toks + h * rows + r, last
-
     def score(keys, slot):
         sb[slot] = jnp.dot(keys, qt[...], preferred_element_type=jnp.float32)
 
     def hide(k, odd):
-        row, last = place_of(k, odd)
-
-        @pl.when(last > first_row)
-        def _():
-            live = row <= first_row + lax.broadcasted_iota(jnp.int32, (KB, toks), 1)
-            for h in range(heads):
-                cols = pl.ds(h * toks, toks)
-                sb[odd, :, cols] = jnp.where(live, sb[odd, :, cols], NEG)
+        count = 2 * rows if odd else rows
+        start = ((here["y"] % 2 if odd else here["z"]) * 4 + here["x"]) * count
+        own = pl.ds(pl.multiple_of(start, rows), count)
+        m = lax.broadcasted_iota(jnp.int32, (count, toks), 0)
+        y_hi = m // rows if odd else (here["y"] + k) % 4 // 2
+        live = (y_hi * 2 + odd) * rows + m % rows <= lax.broadcasted_iota(jnp.int32, (count, toks), 1)
+        for h in range(heads):
+            cols = pl.ds(h * toks, toks)
+            sb[odd, own, cols] = jnp.where(live, sb[odd, own, cols], NEG)
 
     def score_pre(k, slot):
         prefix("block_landed", k)
@@ -330,14 +320,18 @@
 
         score(new_keys(k, 1), 1)
         soft(new_keys(k, 0), 0)
-        hide(k, 1)
+        @pl.when(i == 0)
+        def _():
+            hide(0, 1)
 
         @pl.when(i < 3)
         def _():
             new("block_landed", k_next)
             score(new_keys(k_next, 0), 0)
             soft(new_keys(k, 1), 1)
-            hide(k_next, 0)
+            @pl.when(i == 2)
+            def _():
+                hide(2, 0)
 
         @pl.when(i == 3)
         def _():

time: 81.5 us -> 73.4 us (0.901)
  Pallas kernels: 77.9 us -> 69.8 us
    pallas_call x1, Pallas kernels: 75.9 us -> 67.8 us  [per_device(): pl.pallas_call(functools.partial(kernel, heads, toks), out_shape=[jax.Sha...]
where the time goes in v5:
time: 73.4 us; the launch traced here: 73.2 us
  Pallas kernels  69.8 us (95%)
  other arithmetic  1.93 us (3%)
  between operations  1.33 us (2%)
    pallas_call x1, Pallas kernels, per_device(): pl.pallas_call(functools.partial(kernel, heads, toks), out_shape=[jax.Sha...  67.8 us
    pallas_call x1, Pallas kernels, per_device(): pl.pallas_call(leave, out_shape=[jax.ShapeDtypeStruct(attended.shape, bf)...  2.01 us

profile of v5, /device:TPU:1, one launch (start us, length us, event | category | flops | bytes accessed | tf_op | source)
XLA Modules:
  0.0 73.2 jit_solution(1707241148362597759)
XLA Ops:
  1.3 0.8 %select_reduce_fusion = s32[128]{0:T(128)S(1)} fusion(s32[256]{0:T(256)} %param.19, s32[128]{0:T(128)S(1)} %fusion.1), kind=kLoop, calls=%fused_computation | loop fusion | flops 98176 | bytes 2048 | tf_op jit(solution)/shard_map/reduce_sum | solution.py:379
  2.2 0.1 broadcast_in_dim.16
  2.3 0.3 multiply_cosine_fusion
  2.6 0.7 %pad_maximum_fusion.tab_ref = f32[128,128]{1,0:T(8,128)} fusion(f32[128,64]{1,0:T(8,128)S(1)} %broadcast_in_dim.16, f32[128,32]{1,0:T(8,128)S(1)} %get-tuple-element.7, f32[128,32]{1,0:T(8,128)S(1)} %get-tuple-element.6), kind=kLoop, calls=%fused_computation.3 | loop fusion | flops 32768 | bytes 131072 | tf_op jit(solution)/shard_map/concatenate | solution.py:381
  3.3 67.8 %latent_attention.1 = (bf16[128,2048]{1,0:T(8,128)(2,1)}, f32[128,576]{1,0:T(8,128)}) custom-call(s32[1]{0:T(128)} %copy.13.len_ref, f32[128,128]{1,0:T(8,128)} %pad_maximum_fusion.tab_ref, f32[1,512]{1,0:T(1,128)} %bitcast.5, bf16[128,1792]{1,0:T(8,128)(2,1)} %tok_hbm.1, bf16[576,1792]{1,0:T(8,128)(2,1)} %bitcast.4, bf16[64,576]{1,0:T(8,128)(2,1)} %pre_hbm.1, ...), custom_call_target="tpu_custom_call" | custom-call | tf_op jit(solution)/shard_map/latent_attention/pallas_call | solution.py:388
  71.2 2.0 %leave.1 = (bf16[128,2048]{1,0:T(8,128)(2,1)}, bf16[8,9216]{1,0:T(8,128)(2,1)}) custom-call(bf16[128,2048]{1,0:T(8,128)(2,1)} %get-tuple-element.4.att_ref, f32[128,576]{1,0:T(8,128)} %get-tuple-element.5.rows_ref), custom_call_target="tpu_custom_call" | custom-call | tf_op jit(solution)/shard_map/leave/pallas_call | solution.py:402
  (4 shorter events, 0.0 us)
